TPU v7x, 512 devices: a whole 4x8x8 slice. The times are simulated.
512 devices in a mesh: contact: 8 (over x, core), body: 8 (over z), group: 8 (over y).
Axes of the slice: x: 4, y: 8, z: 8, core: 2. Of those that a mesh axis runs over, the one named last changes fastest.
Arguments:
- jacobian_a: float32 [18, 1835008], P(None, ('contact', 'body', 'group')), may hold values from -4 to 4
- jacobian_b: float32 [18, 1835008], P(None, ('contact', 'body', 'group')), may hold values from -4 to 4
- warm_start: float32 [3, 1835008], P(None, ('contact', 'body', 'group')), may hold values from -4 to 4
- free_gap: float32 [3, 1835008], P(None, ('contact', 'body', 'group')), may hold values from -25 to 25
- compliance: float32 [3, 1835008], P(None, ('contact', 'body', 'group')), may hold values from 0.05 to 2.5
- friction: float32 [1835008], P(('contact', 'body', 'group')), may hold values from 0.2 to 0.8
- cone_active: int32 [1835008], P(('contact', 'body', 'group')), may hold values 0 or 1
- body_index_a: int32 [1835008], P(('contact', 'body', 'group')), may hold values from 0 to 4095
- body_index_b: int32 [1835008], P(('contact', 'body', 'group')), may hold values from 0 to 4095
- block_owner: int32 [28672, 1], P(('contact', 'body', 'group')), may hold values from 0 to 63; in each aligned block of 56 rows (0 to 55, 56 to 111, ...) at most 2 rows name the same one
- inverse_mass: float32 [6, 262144], P(None, ('body', 'group')), may hold values from 0.3 to 3
- free_velocity: float32 [6, 262144], P(None, ('body', 'group')), may hold values from -6 to 6
Outputs:
- impulse: float32 [3, 1835008], P(None, ('contact', 'body', 'group'))
- velocity: float32 [6, 262144], P(None, ('body', 'group'))
Inputs may be any that keep to these rules, and one draw needn't show every extreme that they name: `block_owner`: in each aligned block of 56 rows (the contact blocks of one device) no shard is named more than 2 times.
All inputs are finite; a program needn't handle non-finite values. No bound on the sum of `cone_active` on one device may be relied on, other than what follows from the above.
Results may differ from a plain program's by a relative error of at most 0.0003.
Values sent between devices are 32-bit elements; how exact they have to be, the bound alone decides.
A program may use at most 64 MiB of HBM per device.

v0:
```python
import math

import jax
import jax.numpy as jnp
from jax import lax
from jax.sharding import Mesh
from jax.sharding import PartitionSpec as P

CBLK = 64
ITERS = 2
CONTACT = ("contact_0", "contact_1")
CONTACT_BODY_GROUP = ("contact_0", "contact_1", "body", "group")


EPS = 1e-06
SMOOTH = 0.1


def copy_for_each(array, axis):
    length = lax.axis_size(axis)
    return lax.all_to_all(
        jnp.broadcast_to(array[None], (length, *array.shape)), axis, 0, 0, tiled=True
    )


def of_everyone(array, axis):
    everything = copy_for_each(array, axis)
    return jnp.sum(everything, axis=0)


def by_axis(array, axes):
    for axis in axes:
        array = lax.psum(array, axis)
    return array


def momentum_table(iterations):
    theta_now = 1.0
    coefficients = []
    for rounds in range(iterations):
        following = 0.5 * (
            theta_now * math.sqrt(theta_now * theta_now + 4.0) - theta_now * theta_now
        )
        coefficients.append(theta_now * (1.0 - theta_now) / (theta_now * theta_now + following))
        theta_now = following
    return coefficients


def project_cone(values, friction, cone_active):
    normal = values[0]
    tangent = values[1:3]
    spread = jnp.sqrt(tangent[0] * tangent[0] + tangent[1] * tangent[1] + SMOOTH * SMOOTH)
    sticking = spread <= friction * normal
    separated = friction * spread <= -normal
    cone_normal = (normal + friction * spread) / (1.0 + friction * friction)
    shrink_factor = friction * cone_normal / spread
    new_normal = jnp.where(sticking, normal, jnp.where(separated, 0.0, cone_normal))
    new_tangent = jnp.where(
        sticking[None], tangent, jnp.where(separated[None], 0.0, shrink_factor[None] * tangent)
    )
    switched = cone_active == 1
    out_normal = jnp.where(switched, new_normal, jnp.maximum(normal, 0.0))
    out_tangent = jnp.where(switched[None], new_tangent, 0.0)
    return jnp.concatenate([out_normal[None], out_tangent], axis=0)


def impulse_terms(jacobian, values):
    return jnp.sum(jacobian.reshape(3, 6, -1) * values[:, None, :], axis=0)


def velocity_terms(jacobian, velocities):
    return jnp.sum(jacobian.reshape(3, 6, -1) * velocities[None, :, :], axis=1)


def slot_places(block_owner, capacity):
    target = block_owner[:, 0]
    matching = (target[:, None] == target[None, :]).astype(jnp.int32)
    ordinal = jnp.arange(target.shape[0], dtype=jnp.int32)
    earlier = (ordinal[None, :] < ordinal[:, None]).astype(jnp.int32)
    ranking = jnp.sum(matching * earlier, axis=1)
    return target * capacity + ranking


def pack_slots(values, places, shards, capacity):
    leading = values.shape[0]
    blocks = values.reshape(leading, -1, CBLK)
    buffer = jnp.zeros((leading, shards * capacity, CBLK), values.dtype)
    buffer = buffer.at[:, places, :].set(blocks)
    return buffer.reshape(leading, shards, capacity * CBLK)


def unpack_slots(buffer, places):
    leading = buffer.shape[0]
    blocks = buffer.reshape(leading, -1, CBLK)[:, places, :]
    return blocks.reshape(leading, -1)


def trade(buffer):
    return lax.all_to_all(buffer, ("body", "group"), split_axis=1, concat_axis=1, tiled=True)


def on_device(
    jacobian_a,
    jacobian_b,
    warm_start,
    free_gap,
    compliance,
    friction,
    cone_active,
    body_index_a,
    body_index_b,
    block_owner,
    inverse_mass,
    free_velocity,
):
    shards = lax.axis_size(("body", "group"))
    capacity = max(2, 2 * block_owner.shape[0] // shards)
    places = slot_places(block_owner, capacity)
    bodies = inverse_mass.shape[1]
    index_slots = pack_slots(body_index_b[None, :], places, shards, capacity)
    far_index = lax.all_to_all(
        index_slots, ("body", "group"), split_axis=1, concat_axis=1, tiled=True
    ).reshape(-1)

    def body_impulse(values):
        summed = (
            jnp.zeros((6, bodies), jnp.float32)
            .at[:, body_index_a]
            .add(impulse_terms(jacobian_a, values))
        )
        far_terms = trade(
            pack_slots(impulse_terms(jacobian_b, values), places, shards, capacity)
        ).reshape(6, -1)
        summed = summed.at[:, far_index].add(far_terms)
        return of_everyone(summed, CONTACT)

    momentum = momentum_table(ITERS)
    current = warm_start
    before = jnp.zeros_like(warm_start)
    gradient_before = free_gap
    latest = warm_start
    for rounds in range(ITERS):
        velocities = inverse_mass * body_impulse(current)
        near_part = velocity_terms(jacobian_a, velocities[:, body_index_a])
        returned = trade(velocities[:, far_index].reshape(6, shards, -1))
        gradient = (
            near_part
            + velocity_terms(jacobian_b, unpack_slots(returned, places))
            + compliance * current
            + free_gap
        )
        iterate_change = current - before
        gradient_change = gradient - gradient_before
        change_squares, gradient_squares = (
            by_axis(jnp.sum(iterate_change * iterate_change), CONTACT_BODY_GROUP),
            by_axis(jnp.sum(gradient_change * gradient_change), CONTACT_BODY_GROUP),
        )
        stride = jnp.sqrt((change_squares + EPS) / (gradient_squares + EPS))
        projected = project_cone(current - stride * gradient, friction, cone_active)
        following = projected + momentum[rounds] * (projected - latest)
        before, gradient_before, latest, current = (current, gradient, projected, following)
    velocity = free_velocity + inverse_mass * body_impulse(latest)
    return (latest, velocity)


def solution(mesh):
    torus = Mesh(
        mesh.devices.reshape(4, 2, mesh.shape["body"], mesh.shape["group"]),
        ("contact_0", "contact_1", "body", "group"),
    )
    placed = (
        P(None, CONTACT_BODY_GROUP),
        P(None, CONTACT_BODY_GROUP),
        P(None, CONTACT_BODY_GROUP),
        P(None, CONTACT_BODY_GROUP),
        P(None, CONTACT_BODY_GROUP),
        P(CONTACT_BODY_GROUP),
        P(CONTACT_BODY_GROUP),
        P(CONTACT_BODY_GROUP),
        P(CONTACT_BODY_GROUP),
        P(CONTACT_BODY_GROUP, None),
        P(None, ("body", "group")),
        P(None, ("body", "group")),
    )
    return jax.shard_map(
        on_device,
        mesh=torus,
        in_specs=placed,
        out_specs=(P(None, CONTACT_BODY_GROUP), P(None, ("body", "group"))),
        check_vma=False,
    )
```

profile of v0, /device:TPU:1, one launch (start us, length us, event | category | flops | bytes accessed | tf_op | source)
XLA Modules:
  0.0 576.8 jit_solution(6024349499058837542)
XLA Ops:
  4.4 17.1 %all-to-all-start = ((s32[1,64,128]{2,0,1:T(1,128)}), s32[1,64,128]{2,0,1:T(1,128)S(1)}, u32[]{:S(2)}, u32[]{:S(2)}) async-start(s32[1,64,128]{2,0,1:T(1,128)} %bitcast.4), calls=%async_computation | async-start | bytes 65536 | tf_op jit(solution)/shard_map/all_to_all | solution.py:121
  30.8 20.5 %scatter_custom_fusion = f32[6,4096]{0,1:T(8,128)S(1)} fusion(s32[3584]{0:T(1024)S(1)} %compare_select_fusion.1, f32[3584,6]{1,0:T(8,128)} %copy.192, f32[]{:T(128)} %constant.10.clone.1), kind=kCustom, calls=%fused_computation.20 | custom fusion | flops 21504 | bytes 98816 | tf_op jit(solution)/shard_map/scatter-add | solution.py:129
  51.3 12.1 %all-to-all-start.1 = ((f32[6,64,128]{2,0,1:T(8,128)}), f32[6,64,128]{2,0,1:T(8,128)S(1)}, u32[]{:S(2)}, u32[]{:S(2)}) async-start(f32[6,64,128]{2,0,1:T(8,128)} %copy.196), calls=%async_computation.1 | async-start | bytes 524288 | tf_op jit(solution)/shard_map/all_to_all | solution.py:99
  63.5 12.4 %all-to-all-done.1 = f32[6,64,128]{2,0,1:T(8,128)S(1)} async-done(((f32[6,64,128]{2,0,1:T(8,128)}), f32[6,64,128]{2,0,1:T(8,128)S(1)}, u32[]{:S(2)}, u32[]{:S(2)}) %all-to-all-start.1) | async-done | bytes 196640 | tf_op jit(solution)/shard_map/all_to_all | solution.py:99
  78.5 51.9 %scatter_fusion.1 = f32[6,4096]{0,1:T(8,128)S(1)} fusion(f32[6,4096]{0,1:T(8,128)S(1)} %scatter_custom_fusion, s32[8192]{0:T(1024)S(1)} %bitcast.43, f32[8192,6]{1,0:T(8,128)} %copy.197), kind=kCustom, calls=%fused_computation.9 | custom fusion | flops 49152 | bytes 622592 | tf_op jit(solution)/shard_map/scatter-add | solution.py:134
  132.1 7.8 %all-to-all-start.2 = ((f32[8,6,4096]{2,1,0:T(8,128)}), f32[8,6,4096]{2,1,0:T(8,128)S(1)}, u32[]{:S(2)}, u32[]{:S(2)}) async-start(f32[8,6,4096]{2,1,0:T(8,128)} %broadcast_in_dim.66), calls=%async_computation.2 | async-start | bytes 2097152 | tf_op jit(solution)/shard_map/all_to_all | solution.py:21
  139.9 15.1 %all-to-all-done.2 = f32[8,6,4096]{2,1,0:T(8,128)S(1)} async-done(((f32[8,6,4096]{2,1,0:T(8,128)}), f32[8,6,4096]{2,1,0:T(8,128)S(1)}, u32[]{:S(2)}, u32[]{:S(2)}) %all-to-all-start.2) | async-done | bytes 786464 | tf_op jit(solution)/shard_map/all_to_all | solution.py:21
  155.7 27.7 %gather_fusion.1 = f32[8192,6]{1,0:T(8,128)} fusion(f32[6,4096]{0,1:T(8,128)S(1)} %copy.200, s32[8192]{0:T(1024)S(1)} %broadcast_clamp_fusion), kind=kCustom, calls=%fused_computation.1 | custom fusion | bytes 425984 | tf_op jit(solution)/shard_map/gather | solution.py:145
  206.7 7.5 %all-reduce.5 = (f32[]{:T(128)}, f32[]{:T(128)}) all-reduce(f32[]{:T(128)} %get-tuple-element.40, f32[]{:T(128)} %get-tuple-element.38), channel_id=1, replica_groups=mesh['contact_0'=4,'contact_1'=2,'body'=8,'group'=8] {'contact_0'}, use_global_device_ids=true, to_apply=%region_1.0 | all-reduce | flops 2 | bytes 16 | tf_op jit(solution)/shard_map/psum | solution.py:33
  214.2 8.1 %all-reduce.7 = (f32[]{:T(128)}, f32[]{:T(128)}) all-reduce(f32[]{:T(128)} %get-tuple-element.22, f32[]{:T(128)} %get-tuple-element.23), channel_id=1, replica_groups=mesh['contact_0'=4,'contact_1'=2,'body'=8,'group'=8] {'contact_1'}, use_global_device_ids=true, to_apply=%region_2.0 | all-reduce | flops 2 | bytes 16 | tf_op jit(solution)/shard_map/psum | solution.py:33
  222.3 11.6 %all-reduce.3 = (f32[]{:T(128)}, f32[]{:T(128)}) all-reduce(f32[]{:T(128)} %get-tuple-element.26, f32[]{:T(128)} %get-tuple-element.27), channel_id=1, replica_groups=mesh['contact_0'=4,'contact_1'=2,'body'=8,'group'=8] {'body'}, use_global_device_ids=true, to_apply=%region_3.0 | all-reduce | flops 2 | bytes 16 | tf_op jit(solution)/shard_map/psum | solution.py:33
  233.9 12.2 %all-reduce.1 = (f32[]{:T(128)}, f32[]{:T(128)}) all-reduce(f32[]{:T(128)} %get-tuple-element.18, f32[]{:T(128)} %get-tuple-element.19), channel_id=1, replica_groups=mesh['contact_0'=4,'contact_1'=2,'body'=8,'group'=8] {'group'}, use_global_device_ids=true, to_apply=%region_4.0 | all-reduce | flops 2 | bytes 16 | tf_op jit(solution)/shard_map/psum | solution.py:33
  261.4 20.5 %scatter_custom_fusion.4 = f32[6,4096]{0,1:T(8,128)S(1)} fusion(s32[3584]{0:T(1024)S(1)} %compare_select_fusion.1, f32[3584,6]{1,0:T(8,128)} %copy.207, f32[]{:T(128)} %constant.10.clone.1), kind=kCustom, calls=%fused_computation.18 | custom fusion | flops 21504 | bytes 98816 | tf_op jit(solution)/shard_map/scatter-add | solution.py:129
  284.5 51.9 %scatter_fusion.3 = f32[6,4096]{0,1:T(8,128)S(1)} fusion(f32[6,4096]{0,1:T(8,128)S(1)} %scatter_custom_fusion.4, s32[8192]{0:T(1024)S(1)} %bitcast.45, f32[8192,6]{1,0:T(8,128)} %copy.211), kind=kCustom, calls=%fused_computation.12 | custom fusion | flops 49152 | bytes 622592 | tf_op jit(solution)/shard_map/scatter-add | solution.py:134
  337.1 25.5 %all_to_all.45 = f32[8,6,4096]{2,1,0:T(8,128)S(1)} all-to-all(f32[8,6,4096]{2,1,0:T(8,128)S(1)} %broadcast_in_dim.122), channel_id=1, replica_groups=mesh['contact_0'=4,'contact_1'=2,'body'=8,'group'=8] {'contact_0','conta..., dimensions={0} | all-to-all | bytes 1572864 | tf_op jit(solution)/shard_map/all_to_all | solution.py:21
  363.3 27.7 %gather_fusion.4 = f32[8192,6]{1,0:T(8,128)} fusion(f32[6,4096]{0,1:T(8,128)S(1)} %copy.214, s32[8192]{0:T(1024)S(1)} %broadcast_clamp_fusion), kind=kCustom, calls=%fused_computation.4 | custom fusion | bytes 425984 | tf_op jit(solution)/shard_map/gather | solution.py:145
  394.5 11.9 %all-to-all-start.6 = ((f32[6,64,128]{2,0,1:T(8,128)}), f32[6,64,128]{2,0,1:T(8,128)S(1)}, u32[]{:S(2)}, u32[]{:S(2)}) async-start(f32[6,64,128]{2,0,1:T(8,128)} %copy.217), calls=%async_computation.6 | async-start | bytes 524288 | tf_op jit(solution)/shard_map/all_to_all | solution.py:99
  420.6 7.5 %all-reduce.4 = (f32[]{:T(128)}, f32[]{:T(128)}) all-reduce(f32[]{:T(128)} %get-tuple-element.33, f32[]{:T(128)} %get-tuple-element.31), channel_id=1, replica_groups=mesh['contact_0'=4,'contact_1'=2,'body'=8,'group'=8] {'contact_0'}, use_global_device_ids=true, to_apply=%region_21.22 | all-reduce | flops 2 | bytes 16 | tf_op jit(solution)/shard_map/psum | solution.py:33
  428.1 8.2 %all-reduce.6 = (f32[]{:T(128)}, f32[]{:T(128)}) all-reduce(f32[]{:T(128)} %get-tuple-element.20, f32[]{:T(128)} %get-tuple-element.21), channel_id=1, replica_groups=mesh['contact_0'=4,'contact_1'=2,'body'=8,'group'=8] {'contact_1'}, use_global_device_ids=true, to_apply=%region_22.23 | all-reduce | flops 2 | bytes 16 | tf_op jit(solution)/shard_map/psum | solution.py:33
  436.3 11.6 %all-reduce.2 = (f32[]{:T(128)}, f32[]{:T(128)}) all-reduce(f32[]{:T(128)} %get-tuple-element.24, f32[]{:T(128)} %get-tuple-element.25), channel_id=1, replica_groups=mesh['contact_0'=4,'contact_1'=2,'body'=8,'group'=8] {'body'}, use_global_device_ids=true, to_apply=%region_23.24 | all-reduce | flops 2 | bytes 16 | tf_op jit(solution)/shard_map/psum | solution.py:33
  448.0 12.2 %all-reduce = (f32[]{:T(128)}, f32[]{:T(128)}) all-reduce(f32[]{:T(128)} %get-tuple-element.16, f32[]{:T(128)} %get-tuple-element.17), channel_id=1, replica_groups=mesh['contact_0'=4,'contact_1'=2,'body'=8,'group'=8] {'group'}, use_global_device_ids=true, to_apply=%region_24.25 | all-reduce | flops 2 | bytes 16 | tf_op jit(solution)/shard_map/psum | solution.py:33
  474.9 20.5 %scatter_custom_fusion.7 = f32[6,4096]{0,1:T(8,128)S(1)} fusion(s32[3584]{0:T(1024)S(1)} %compare_select_fusion.1, f32[3584,6]{1,0:T(8,128)} %copy.221, f32[]{:T(128)} %constant.10.clone.1), kind=kCustom, calls=%fused_computation.16 | custom fusion | flops 21504 | bytes 98816 | tf_op jit(solution)/shard_map/scatter-add | solution.py:129
  498.0 51.9 %scatter_fusion.5 = f32[6,4096]{0,1:T(8,128)S(1)} fusion(f32[6,4096]{0,1:T(8,128)S(1)} %scatter_custom_fusion.7, s32[8192]{0:T(1024)S(1)} %bitcast.46, f32[8192,6]{1,0:T(8,128)} %copy.225), kind=kCustom, calls=%fused_computation.15 | custom fusion | flops 49152 | bytes 622592 | tf_op jit(solution)/shard_map/scatter-add | solution.py:134
  550.6 25.5 %all_to_all.46 = f32[8,6,4096]{2,1,0:T(8,128)S(1)} all-to-all(f32[8,6,4096]{2,1,0:T(8,128)S(1)} %broadcast_in_dim.126), channel_id=1, replica_groups=mesh['contact_0'=4,'contact_1'=2,'body'=8,'group'=8] {'contact_0','conta..., dimensions={0} | all-to-all | bytes 1572864 | tf_op jit(solution)/shard_map/all_to_all | solution.py:21
  (116 shorter events, 94.0 us)
Async XLA Ops:
  4.4 46.8 %all-to-all-start = ((s32[1,64,128]{2,0,1:T(1,128)}), s32[1,64,128]{2,0,1:T(1,128)S(1)}, u32[]{:S(2)}, u32[]{:S(2)}) async-start(s32[1,64,128]{2,0,1:T(1,128)} %bitcast.4), calls=%async_computation | async-start | bytes 65536 | tf_op jit(solution)/shard_map/all_to_all | solution.py:121
  51.3 24.6 %all-to-all-start.1 = ((f32[6,64,128]{2,0,1:T(8,128)}), f32[6,64,128]{2,0,1:T(8,128)S(1)}, u32[]{:S(2)}, u32[]{:S(2)}) async-start(f32[6,64,128]{2,0,1:T(8,128)} %copy.196), calls=%async_computation.1 | async-start | bytes 524288 | tf_op jit(solution)/shard_map/all_to_all | solution.py:99
  131.0 24.0 %copy-start = (f32[6,4096]{1,0:T(8,128)S(1)}, f32[6,4096]{1,0:T(8,128)}, u32[]{:S(2)}) copy-start(f32[6,4096]{1,0:T(8,128)} %param.22) | copy-start | bytes 294916
  132.1 22.9 %all-to-all-start.2 = ((f32[8,6,4096]{2,1,0:T(8,128)}), f32[8,6,4096]{2,1,0:T(8,128)S(1)}, u32[]{:S(2)}, u32[]{:S(2)}) async-start(f32[8,6,4096]{2,1,0:T(8,128)} %broadcast_in_dim.66), calls=%async_computation.2 | async-start | bytes 2097152 | tf_op jit(solution)/shard_map/all_to_all | solution.py:21
  186.9 17.6 %all-to-all-start.3 = ((f32[6,64,128]{2,0,1:T(8,128)}), f32[6,64,128]{2,0,1:T(8,128)S(1)}, u32[]{:S(2)}, u32[]{:S(2)}) async-start(f32[6,64,128]{2,0,1:T(8,128)} %copy.203), calls=%async_computation.3 | async-start | bytes 524288 | tf_op jit(solution)/shard_map/all_to_all | solution.py:99
  201.5 4.5 copy-start.1
  201.5 4.5 copy-start.2
  201.5 4.5 copy-start.3
  204.6 43.1 %copy-start.5 = (f32[3584]{0:T(1024)S(1)}, f32[3584]{0:T(1024)}, u32[]{:S(2)}) copy-start(f32[3584]{0:T(1024)} %param.17) | copy-start | bytes 43012
  204.6 43.1 %copy-start.7 = (s32[3584]{0:T(1024)S(1)}, s32[3584]{0:T(1024)}, u32[]{:S(2)}) copy-start(s32[3584]{0:T(1024)} %param.18) | copy-start | bytes 43012
  252.2 29.6 %all-to-all-start.4 = ((f32[6,64,128]{2,0,1:T(8,128)}), f32[6,64,128]{2,0,1:T(8,128)S(1)}, u32[]{:S(2)}, u32[]{:S(2)}) async-start(f32[6,64,128]{2,0,1:T(8,128)} %copy.210), calls=%async_computation.4 | async-start | bytes 524288 | tf_op jit(solution)/shard_map/all_to_all | solution.py:99
  394.5 24.2 %all-to-all-start.6 = ((f32[6,64,128]{2,0,1:T(8,128)}), f32[6,64,128]{2,0,1:T(8,128)S(1)}, u32[]{:S(2)}, u32[]{:S(2)}) async-start(f32[6,64,128]{2,0,1:T(8,128)} %copy.217), calls=%async_computation.6 | async-start | bytes 524288 | tf_op jit(solution)/shard_map/all_to_all | solution.py:99
  461.9 3.0 copy-start.4
  465.7 29.7 %all-to-all-start.7 = ((f32[6,64,128]{2,0,1:T(8,128)}), f32[6,64,128]{2,0,1:T(8,128)S(1)}, u32[]{:S(2)}, u32[]{:S(2)}) async-start(f32[6,64,128]{2,0,1:T(8,128)} %copy.224), calls=%async_computation.7 | async-start | bytes 524288 | tf_op jit(solution)/shard_map/all_to_all | solution.py:99
  550.5 25.6 %copy-start.6 = (f32[6,4096]{1,0:T(8,128)S(1)}, f32[6,4096]{1,0:T(8,128)}, u32[]{:S(2)}) copy-start(f32[6,4096]{1,0:T(8,128)} %param.23) | copy-start | bytes 294916
where the time goes:
time: 578 us; the launch traced here: 577 us
  other arithmetic  224 us (39%)
  blocking collectives  130 us (22%)
  local copies, waits for them, and re-layouts  116 us (20%)
  starting transfers between devices  68.8 us (12%)
  waiting for transfers between devices  33.2 us (6%)
    scatter-add x3, other arithmetic, body_impulse(): summed = summed.at[:, far_index].add(far_terms)  156 us
    psum x8, blocking collectives, by_axis(): array = lax.psum(array, axis)  79 us
    scatter-add x3, other arithmetic, body_impulse(): summed = jnp.zeros((6, bodies), jnp.float32).at[:, body_index_a].add(impu...  61.4 us
    gather x2, local copies, waits for them, and re-layouts, on_device(): returned = trade(velocities[:, far_index].reshape(6, shards, -1))  55.4 us
    all_to_all x2, blocking collectives, copy_for_each(): lax.all_to_all(jnp.broadcast_to(array[None], (length, *array.shape)), axi...  50.9 us
    all_to_all x5, starting transfers between devices, trade(): lax.all_to_all(buffer, ('body', 'group'), split_axis=1, concat_axis=1, ti...  43.9 us
    gather x4, local copies, waits for them, and re-layouts, on_device(): near_part = velocity_terms(jacobian_a, velocities[:, body_index_a])  18.8 us
    all_to_all x5, waiting for transfers between devices, trade(): lax.all_to_all(buffer, ('body', 'group'), split_axis=1, concat_axis=1, ti...  18.1 us
  transfers between devices with their start and end apart: 7, of which 4 were waited for; matrix products, arithmetic and copies ran while one was open for 16% of the time, Pallas kernels for 0%

commit v1 on v0

v1 whole, which is shorter than its diff:
```python
import math

import jax
import jax.numpy as jnp
from jax import lax
from jax.experimental import pallas as pl
from jax.experimental.pallas import tpu as pltpu
from jax.sharding import Mesh
from jax.sharding import PartitionSpec as P

CBLK = 64
ITERS = 2
CONTACT = ("contact_0", "contact_1")
SHARD = ("body", "group")
CONTACT_BODY_GROUP = ("contact_0", "contact_1", "body", "group")

EPS = 1e-06
SMOOTH = 0.1

LANES = 256
ROWS = 16
CHUNK = 512
WIDE = CHUNK // 128

VMEM = pl.BlockSpec(memory_space=pltpu.VMEM)
SMEM = pl.BlockSpec(memory_space=pltpu.SMEM)


def momentum_table(iterations):
    theta_now = 1.0
    coefficients = []
    for rounds in range(iterations):
        following = 0.5 * (
            theta_now * math.sqrt(theta_now * theta_now + 4.0) - theta_now * theta_now
        )
        coefficients.append(theta_now * (1.0 - theta_now) / (theta_now * theta_now + following))
        theta_now = following
    return coefficients


def slot_places(block_owner, capacity):
    target = block_owner[:, 0]
    matching = (target[:, None] == target[None, :]).astype(jnp.int32)
    ordinal = jnp.arange(target.shape[0], dtype=jnp.int32)
    earlier = (ordinal[None, :] < ordinal[:, None]).astype(jnp.int32)
    ranking = jnp.sum(matching * earlier, axis=1)
    return target * capacity + ranking


def exchange(array, axes):
    return lax.all_to_all(array, axes, 0, 0, tiled=True)


def impulse_rows(jacobian, values):
    total = jacobian[0:6] * values[0:1]
    for r in range(1, 3):
        total = total + jacobian[6 * r : 6 * r + 6] * values[r : r + 1]
    return total


def velocity_rows(jacobian, velocities):
    rows = [
        jnp.sum(jacobian[6 * r : 6 * r + 6] * velocities, axis=0, keepdims=True)
        for r in range(3)
    ]
    return jnp.concatenate(rows, axis=0)


def lane_onehot(index):
    lane = index & (LANES - 1)
    iota = lax.broadcasted_iota(jnp.int32, (LANES, index.shape[1]), 0)
    return jnp.where(iota == lane, 1.0, 0.0).astype(jnp.bfloat16)


def row_mask(index):
    iota = lax.broadcasted_iota(jnp.int32, (ROWS, index.shape[1]), 0)
    return iota == (index >> 8)


def pair(values):
    high = values.astype(jnp.bfloat16).astype(jnp.float32)
    return high, values - high


def scatter_chunk(acc_ref, terms, index):
    mask = row_mask(index)
    high, low = pair(terms)
    parts = [jnp.where(mask, part[c : c + 1], 0.0) for part in (high, low) for c in range(6)]
    spread = jnp.concatenate(parts, axis=0).astype(jnp.bfloat16)
    acc_ref[...] += lax.dot_general(
        spread,
        lane_onehot(index),
        (((1,), (1,)), ((), ())),
        preferred_element_type=jnp.float32,
    )


def gather_chunk(table, index):
    mask = row_mask(index)
    found = jnp.dot(table, lane_onehot(index), preferred_element_type=jnp.float32)
    found = found[: 6 * ROWS] + found[6 * ROWS :]
    rows = [
        jnp.sum(jnp.where(mask, found[ROWS * c : ROWS * (c + 1)], 0.0), axis=0, keepdims=True)
        for c in range(6)
    ]
    return rows


def pack_rows(places_ref, packed, out_ref):
    out_ref[...] = jnp.zeros_like(out_ref)
    lane = lax.broadcasted_iota(jnp.int32, (8, 128), 1)
    for i in range(packed.shape[1] // 128):
        tile = packed[:, 128 * i : 128 * (i + 1)]
        turned = pltpu.roll(tile, 64, 1)
        for h in range(2):
            place = places_ref[2 * i + h]
            shard, half = place >> 1, place & 1
            moved = jnp.where(jnp.full((8, 128), half, jnp.int32) == h, tile, turned)
            out_ref[shard] = jnp.where((lane >> 6) == half, moved, out_ref[shard])


def unpack_tile(places_ref, ret_ref, i):
    lane = lax.broadcasted_iota(jnp.int32, (8, 128), 1)
    moved = []
    for h in range(2):
        place = places_ref[2 * i + h]
        shard, half = place >> 1, place & 1
        tile = ret_ref[shard]
        turned = pltpu.roll(tile, 64, 1)
        moved.append(jnp.where(jnp.full((8, 128), half, jnp.int32) == h, tile, turned))
    return jnp.where(lane < 64, moved[0], moved[1])


def packed_terms(jacobian, values, index):
    count = values.shape[1]
    return jnp.concatenate(
        [
            impulse_rows(jacobian, values),
            index.astype(jnp.float32),
            jnp.zeros((1, count), jnp.float32),
        ],
        axis=0,
    )


def pack_kernel(places_ref, jb_ref, y_ref, ib_ref, out_ref):
    pack_rows(places_ref, packed_terms(jb_ref[...], y_ref[...], ib_ref[...]), out_ref)


def scatter_kernel(recv_ref, ja_ref, y_ref, ia_ref, out_ref, near_ref, acc_ref):
    near_ref[...] = impulse_rows(ja_ref[...], y_ref[...])
    acc_ref[...] = jnp.zeros_like(acc_ref)

    def far(i, carry):
        tiles = [recv_ref[WIDE * i + k] for k in range(WIDE)]
        both = jnp.concatenate(tiles, axis=1)
        scatter_chunk(acc_ref, both[0:6], both[6:7].astype(jnp.int32))
        return carry

    lax.fori_loop(0, recv_ref.shape[0] // WIDE, far, 0)

    def near(i, carry):
        at = pl.ds(pl.multiple_of(i * CHUNK, CHUNK), CHUNK)
        scatter_chunk(acc_ref, near_ref[:, at], ia_ref[:, at])
        return carry

    lax.fori_loop(0, ia_ref.shape[1] // CHUNK, near, 0)
    for t in range(24):
        g, half = t // 2, t % 2
        at = slice(128 * half, 128 * half + 128)
        out_ref[t // 3, 8 * (t % 3) : 8 * (t % 3) + 8, :] = (
            acc_ref[8 * g : 8 * g + 8, at] + acc_ref[96 + 8 * g : 104 + 8 * g, at]
        )


def gather_kernel(full_ref, mass_ref, recv_ref, ia_ref, ja_ref, ret_ref, near_ref, tab_ref, va_ref):
    groups = []
    for g in range(12):
        halves = []
        for half in range(2):
            t = 2 * g + half
            at = slice(8 * (t % 3), 8 * (t % 3) + 8)
            halves.append(full_ref[t // 3, at, :] * mass_ref[t // 3, at, :])
        groups.append(jnp.concatenate(halves, axis=1))
    velocities = jnp.concatenate(groups, axis=0)
    high, low = pair(velocities)
    tab_ref[...] = jnp.concatenate([high, low], axis=0).astype(jnp.bfloat16)
    pad = jnp.zeros((2, CHUNK), jnp.float32)

    def far(i, carry):
        tiles = [recv_ref[WIDE * i + k, 6:7, :] for k in range(WIDE)]
        index = jnp.concatenate(tiles, axis=1).astype(jnp.int32)
        rows = jnp.concatenate(gather_chunk(tab_ref[...], index) + [pad], axis=0)
        for k in range(WIDE):
            ret_ref[WIDE * i + k] = rows[:, 128 * k : 128 * (k + 1)]
        return carry

    lax.fori_loop(0, recv_ref.shape[0] // WIDE, far, 0)

    def near(i, carry):
        at = pl.ds(pl.multiple_of(i * CHUNK, CHUNK), CHUNK)
        rows = gather_chunk(tab_ref[...], ia_ref[:, at]) + [pad]
        va_ref[:, at] = jnp.concatenate(rows, axis=0)
        return carry

    lax.fori_loop(0, ia_ref.shape[1] // CHUNK, near, 0)
    near_ref[...] = velocity_rows(ja_ref[...], va_ref[0:6, :])


def gradient_kernel(
    places_ref, ret_ref, near_ref, jb_ref, comp_ref, gap_ref, y_ref, yp_ref, gp_ref,
    g_ref, sums_ref, vb_ref,
):
    count = y_ref.shape[1]
    for i in range(count // 128):
        vb_ref[:, 128 * i : 128 * (i + 1)] = unpack_tile(places_ref, ret_ref, i)
    gradient = (
        near_ref[...]
        + velocity_rows(jb_ref[...], vb_ref[0:6, :])
        + comp_ref[...] * y_ref[...]
        + gap_ref[...]
    )
    g_ref[...] = gradient
    change = y_ref[...] - yp_ref[...]
    slope = gradient - gp_ref[...]
    rows = []
    for square in (change * change, slope * slope):
        row = jnp.sum(square, axis=0, keepdims=True)
        total = row[:, 0:128]
        for i in range(1, count // 128):
            total = total + row[:, 128 * i : 128 * (i + 1)]
        rows.append(total)
    rows.append(jnp.zeros((6, 128), jnp.float32))
    sums_ref[...] = jnp.concatenate(rows, axis=0)


def step_kernel(
    momentum, places_ref, sums_ref, y_ref, g_ref, xp_ref, mu_ref, act_ref, jb_ref, ib_ref,
    x_ref, yn_ref, out_ref,
):
    total = jnp.sum(sums_ref[...], axis=0)
    total = jnp.sum(total, axis=1, keepdims=True)
    stride = jnp.sqrt((total[0:1] + EPS) / (total[1:2] + EPS))
    z = y_ref[...] - stride * g_ref[...]
    mu = mu_ref[...]
    normal, t1, t2 = z[0:1], z[1:2], z[2:3]
    spread = jnp.sqrt(t1 * t1 + t2 * t2 + SMOOTH * SMOOTH)
    sticking = spread <= mu * normal
    separated = mu * spread <= -normal
    cone_normal = (normal + mu * spread) / (1.0 + mu * mu)
    shrink = mu * cone_normal / spread
    active = act_ref[...] == 1
    out_n = jnp.where(sticking, normal, jnp.where(separated, 0.0, cone_normal))
    out_n = jnp.where(active, out_n, jnp.maximum(normal, 0.0))
    rows = [out_n]
    for t in (t1, t2):
        kept = jnp.where(sticking, t, jnp.where(separated, 0.0, shrink * t))
        rows.append(jnp.where(active, kept, 0.0))
    projected = jnp.concatenate(rows, axis=0)
    x_ref[...] = projected
    following = projected + momentum * (projected - xp_ref[...])
    yn_ref[...] = following
    pack_rows(places_ref, packed_terms(jb_ref[...], following, ib_ref[...]), out_ref)


def f32(*shape):
    return jax.ShapeDtypeStruct(shape, jnp.float32)


def on_device(
    jacobian_a,
    jacobian_b,
    warm_start,
    free_gap,
    compliance,
    friction,
    cone_active,
    body_index_a,
    body_index_b,
    block_owner,
    inverse_mass,
    free_velocity,
):
    shards = lax.axis_size(SHARD)
    sharers = lax.axis_size(CONTACT)
    count = warm_start.shape[1]
    places = slot_places(block_owner, 2)
    index_a = body_index_a[None, :]
    index_b = body_index_b[None, :]
    mu = friction[None, :]
    active = cone_active[None, :]
    mass = (
        inverse_mass.reshape(12, 8, 2, 128).transpose(0, 2, 1, 3).reshape(sharers, 24, 128)
    )

    pack = pl.pallas_call(
        pack_kernel,
        out_shape=f32(shards, 8, 128),
        in_specs=[SMEM, VMEM, VMEM, VMEM],
        out_specs=VMEM,
    )
    scatter = pl.pallas_call(
        scatter_kernel,
        out_shape=f32(sharers, 24, 128),
        in_specs=[VMEM] * 4,
        out_specs=VMEM,
        scratch_shapes=[
            pltpu.VMEM((6, count), jnp.float32),
            pltpu.VMEM((12 * ROWS, LANES), jnp.float32),
        ],
    )
    gather = pl.pallas_call(
        gather_kernel,
        out_shape=(f32(shards, 8, 128), f32(3, count)),
        in_specs=[VMEM] * 5,
        out_specs=(VMEM, VMEM),
        scratch_shapes=[
            pltpu.VMEM((12 * ROWS, LANES), jnp.bfloat16),
            pltpu.VMEM((8, count), jnp.float32),
        ],
    )
    gradient_call = pl.pallas_call(
        gradient_kernel,
        out_shape=(f32(3, count), f32(8, 128)),
        in_specs=[SMEM] + [VMEM] * 8,
        out_specs=(VMEM, VMEM),
        scratch_shapes=[pltpu.VMEM((8, count), jnp.float32)],
    )

    def body_impulse(received, values):
        partial = exchange(scatter(received, jacobian_a, values, index_a), CONTACT)
        mine = jnp.sum(partial, axis=0)
        return exchange(jnp.broadcast_to(mine[None], (sharers, *mine.shape)), CONTACT)

    momentum = momentum_table(ITERS)
    current = warm_start
    before = jnp.zeros_like(warm_start)
    gradient_before = free_gap
    latest = warm_start
    packed = pack(places, jacobian_b, warm_start, index_b)
    for rounds in range(ITERS):
        received = exchange(packed, SHARD)
        full = body_impulse(received, current)
        returned, near = gather(full, mass, received, index_a, jacobian_a)
        gradient, sums = gradient_call(
            places, exchange(returned, SHARD), near, jacobian_b, compliance, free_gap,
            current, before, gradient_before,
        )
        sums = exchange(jnp.broadcast_to(sums[None], (sharers, 8, 128)), CONTACT)
        sums = jnp.sum(sums, axis=0)
        sums = exchange(jnp.broadcast_to(sums[None], (shards, 8, 128)), SHARD)
        last = rounds == ITERS - 1
        step = pl.pallas_call(
            lambda *refs, m=0.0 if last else momentum[rounds]: step_kernel(m, *refs),
            out_shape=(f32(3, count), f32(3, count), f32(shards, 8, 128)),
            in_specs=[SMEM] + [VMEM] * 8,
            out_specs=(VMEM, VMEM, VMEM),
        )
        projected, following, packed = step(
            places, sums, current, gradient, latest, mu, active, jacobian_b, index_b
        )
        before, gradient_before, latest, current = current, gradient, projected, following
    full = body_impulse(exchange(packed, SHARD), latest)
    total = full.reshape(12, 2, 8, 128).transpose(0, 2, 1, 3).reshape(inverse_mass.shape)
    velocity = free_velocity + inverse_mass * total
    return (latest, velocity)


def solution(mesh):
    torus = Mesh(
        mesh.devices.reshape(4, 2, mesh.shape["body"], mesh.shape["group"]),
        ("contact_0", "contact_1", "body", "group"),
    )
    placed = (
        P(None, CONTACT_BODY_GROUP),
        P(None, CONTACT_BODY_GROUP),
        P(None, CONTACT_BODY_GROUP),
        P(None, CONTACT_BODY_GROUP),
        P(None, CONTACT_BODY_GROUP),
        P(CONTACT_BODY_GROUP),
        P(CONTACT_BODY_GROUP),
        P(CONTACT_BODY_GROUP),
        P(CONTACT_BODY_GROUP),
        P(CONTACT_BODY_GROUP, None),
        P(None, ("body", "group")),
        P(None, ("body", "group")),
    )
    return jax.shard_map(
        on_device,
        mesh=torus,
        in_specs=placed,
        out_specs=(P(None, CONTACT_BODY_GROUP), P(None, ("body", "group"))),
        check_vma=False,
    )
```

time: 578 us -> 283 us (0.49)
  other arithmetic: 224 us -> 1.51 us
  local copies, waits for them, and re-layouts: 116 us -> 11 us
  Pallas kernels: 0 us -> 49.9 us
  starting transfers between devices: 68.8 us -> 26.1 us
  blocking collectives: 130 us -> 164 us
    scatter-add x6 -> x0, other arithmetic: 217 us -> none  [the longest x3 156 us: body_impulse(): summed = summed.at[:, far_index].add(far_terms)]
    all_to_all x2 -> x12, blocking collectives: 50.9 us -> 164 us  [exchange(): return lax.all_to_all(array, axes, 0, 0, tiled=True)]
    psum x8 -> x0, blocking collectives: 79 us -> none  [by_axis(): array = lax.psum(array, axis)]
    gather x10 -> x0, local copies, waits for them, and re-layouts: 75.5 us -> none  [the longest x2 55.4 us: on_device(): returned = trade(velocities[:, far_index].reshape(6, shards, -1))]
    pallas_call x0 -> x10, Pallas kernels: none -> 49.9 us  [the longest x3 23.9 us: body_impulse(): partial = exchange(scatter(received, jacobian_a, values, index_a), CONTACT)]
    all_to_all x7 -> x3, starting transfers between devices: 68.8 us -> 26.1 us  [exchange(): return lax.all_to_all(array, axes, 0, 0, tiled=True)]
    reshape x24 -> x3, local copies, waits for them, and re-layouts: 21.5 us -> 0.81 us  [the longest x2 0.73 us: on_device(): inverse_mass.reshape(12, 8, 2, 128).transpose(0, 2, 1, 3)]
    scatter x7 -> x0, local copies, waits for them, and re-layouts: 8.41 us -> none  [pack_slots(): buffer = buffer.at[:, places, :].set(blocks)]
  transfers between devices with their start and end apart: 7 -> 3, of which waited for: 4 -> 3; matrix products, arithmetic and copies ran while one was open for 16% -> 1% of each run, Pallas kernels for 0% -> 0%
where the time goes in v1:
time: 283 us; the launch traced here: 281 us
  blocking collectives  164 us (58%)
  Pallas kernels  49.9 us (18%)
  waiting for transfers between devices  27.9 us (10%)
  starting transfers between devices  26.1 us (9%)
  local copies, waits for them, and re-layouts  11 us (4%)
    all_to_all x12, blocking collectives, exchange(): return lax.all_to_all(array, axes, 0, 0, tiled=True)  164 us
    all_to_all x3, waiting for transfers between devices, exchange(): return lax.all_to_all(array, axes, 0, 0, tiled=True)  27.9 us
    all_to_all x3, starting transfers between devices, exchange(): return lax.all_to_all(array, axes, 0, 0, tiled=True)  26.1 us
    pallas_call x3, Pallas kernels, body_impulse(): partial = exchange(scatter(received, jacobian_a, values, index_a), CONTACT)  23.9 us
    pallas_call x2, Pallas kernels, on_device(): returned, near = gather(full, mass, received, index_a, jacobian_a)  14.7 us
  transfers between devices with their start and end apart: 3, of which 3 were waited for; matrix products, arithmetic and copies ran while one was open for 1% of the time, Pallas kernels for 0%

profile of v1, /device:TPU:1, one launch (start us, length us, event | category | flops | bytes accessed | tf_op | source)
XLA Modules:
  0.0 281.2 jit_solution(9721198084422641644)
XLA Ops:
  5.4 17.3 %all-to-all-start = ((f32[64,8,128]{2,1,0:T(8,128)}), f32[64,8,128]{2,1,0:T(8,128)S(1)}, u32[]{:S(2)}, u32[]{:S(2)}) async-start(f32[64,8,128]{2,1,0:T(8,128)} %shard_map.131), calls=%async_computation | async-start | bytes 524288 | tf_op jit(solution)/shard_map/all_to_all | solution.py:51
  23.3 12.0 %all-to-all-done.recv_ref = f32[64,8,128]{2,1,0:T(8,128)S(1)} async-done(((f32[64,8,128]{2,1,0:T(8,128)}), f32[64,8,128]{2,1,0:T(8,128)S(1)}, u32[]{:S(2)}, u32[]{:S(2)}) %all-to-all-start) | async-done | bytes 262176 | tf_op jit(solution)/shard_map/all_to_all | solution.py:51
  36.0 8.0 %shard_map.132 = f32[8,24,128]{2,1,0:T(8,128)} custom-call(f32[64,8,128]{2,1,0:T(8,128)} %copy-done, f32[18,3584]{1,0:T(8,128)} %ja_ref.9, f32[3,3584]{1,0:T(4,128)} %yp_ref.1, s32[1,3584]{1,0:T(1,128)} %broadcast_in_dim.25.ia_ref), custom_call_target="tpu_custom_call" | custom-call | tf_op jit(solution)/shard_map/pallas_call | solution.py:331
  44.0 12.5 %all_to_all.75 = f32[8,24,128]{2,1,0:T(8,128)S(1)} all-to-all(f32[8,24,128]{2,1,0:T(8,128)} %shard_map.132), channel_id=1, replica_groups=mesh['contact_0'=4,'contact_1'=2,'body'=8,'group'=8] {'contact_0','conta..., dimensions={0} | all-to-all | bytes 196608 | tf_op jit(solution)/shard_map/all_to_all | solution.py:51
  57.1 4.1 %all-to-all-start.2 = ((f32[8,24,128]{2,1,0:T(8,128)}), f32[8,24,128]{2,1,0:T(8,128)S(1)}, u32[]{:S(2)}, u32[]{:S(2)}) async-start(f32[8,24,128]{2,1,0:T(8,128)} %broadcast_in_dim.26), calls=%async_computation.2 | async-start | bytes 196608 | tf_op jit(solution)/shard_map/all_to_all | solution.py:51
  62.0 4.3 %all-to-all-done.2.full_ref = f32[8,24,128]{2,1,0:T(8,128)S(1)} async-done(((f32[8,24,128]{2,1,0:T(8,128)}), f32[8,24,128]{2,1,0:T(8,128)S(1)}, u32[]{:S(2)}, u32[]{:S(2)}) %all-to-all-start.2) | async-done | bytes 98336 | tf_op jit(solution)/shard_map/all_to_all | solution.py:51
  66.9 7.3 %shard_map.133 = (f32[64,8,128]{2,1,0:T(8,128)}, f32[3,3584]{1,0:T(4,128)}) custom-call(f32[8,24,128]{2,1,0:T(8,128)} %copy-done.3, f32[8,24,128]{2,1,0:T(8,128)} %bitcast.8, f32[64,8,128]{2,1,0:T(8,128)} %copy-done, s32[1,3584]{1,0:T(1,128)} %broadcast_in_dim.25.ia_ref, f32[18,3584]{1,0:T(8,128)} %ja_ref.9), custom_call_target="tpu_custom_call" | custom-call | tf_op jit(solution)/shard_map/pallas_call | solution.py:344
  74.2 18.2 %all_to_all.76.ret_ref = f32[64,8,128]{2,1,0:T(8,128)} all-to-all(f32[64,8,128]{2,1,0:T(8,128)} %get-tuple-element.15), channel_id=1, replica_groups=mesh['contact_0'=4,'contact_1'=2,'body'=8,'group'=8] {'body','group'}, dimensions={0} | all-to-all | bytes 524288 | tf_op jit(solution)/shard_map/all_to_all | solution.py:51
  95.8 10.1 %all_to_all.77 = f32[8,8,128]{2,1,0:T(8,128)S(1)} all-to-all(f32[8,8,128]{2,1,0:T(8,128)S(1)} %broadcast_in_dim.28), channel_id=1, replica_groups=mesh['contact_0'=4,'contact_1'=2,'body'=8,'group'=8] {'contact_0','conta..., dimensions={0} | all-to-all | bytes 65536 | tf_op jit(solution)/shard_map/all_to_all | solution.py:51
  106.7 4.7 %all-to-all-start.5 = ((f32[64,8,128]{2,1,0:T(8,128)}), f32[64,8,128]{2,1,0:T(8,128)S(1)}, u32[]{:S(2)}, u32[]{:S(2)}) async-start(f32[64,8,128]{2,1,0:T(8,128)} %broadcast_in_dim.29), calls=%async_computation.5 | async-start | bytes 524288 | tf_op jit(solution)/shard_map/all_to_all | solution.py:51
  112.7 11.6 %all-to-all-done.5.refs_1_ = f32[64,8,128]{2,1,0:T(8,128)S(1)} async-done(((f32[64,8,128]{2,1,0:T(8,128)}), f32[64,8,128]{2,1,0:T(8,128)S(1)}, u32[]{:S(2)}, u32[]{:S(2)}) %all-to-all-start.5) | async-done | bytes 262176 | tf_op jit(solution)/shard_map/all_to_all | solution.py:51
  127.6 18.1 %all_to_all.78.recv_ref = f32[64,8,128]{2,1,0:T(8,128)} all-to-all(f32[64,8,128]{2,1,0:T(8,128)} %get-tuple-element.19), channel_id=1, replica_groups=mesh['contact_0'=4,'contact_1'=2,'body'=8,'group'=8] {'body','group'}, dimensions={0} | all-to-all | bytes 524288 | tf_op jit(solution)/shard_map/all_to_all | solution.py:51
  145.7 8.0 %shard_map.136 = f32[8,24,128]{2,1,0:T(8,128)} custom-call(f32[64,8,128]{2,1,0:T(8,128)} %all_to_all.78.recv_ref, f32[18,3584]{1,0:T(8,128)} %ja_ref.9, f32[3,3584]{1,0:T(4,128)} %get-tuple-element.20.y_ref.refs_2_, s32[1,3584]{1,0:T(1,128)} %broadcast_in_dim.25.ia_ref), custom_call_target="tpu_custom_call" | custom-call | tf_op jit(solution)/shard_map/pallas_call | solution.py:331
  153.7 12.1 %all_to_all.79 = f32[8,24,128]{2,1,0:T(8,128)S(1)} all-to-all(f32[8,24,128]{2,1,0:T(8,128)} %shard_map.136), channel_id=1, replica_groups=mesh['contact_0'=4,'contact_1'=2,'body'=8,'group'=8] {'contact_0','conta..., dimensions={0} | all-to-all | bytes 196608 | tf_op jit(solution)/shard_map/all_to_all | solution.py:51
  165.8 8.9 %all_to_all.80.full_ref = f32[8,24,128]{2,1,0:T(8,128)} all-to-all(f32[8,24,128]{2,1,0:T(8,128)S(1)} %broadcast_in_dim.32), channel_id=1, replica_groups=mesh['contact_0'=4,'contact_1'=2,'body'=8,'group'=8] {'contact_0','conta..., dimensions={0} | all-to-all | bytes 196608 | tf_op jit(solution)/shard_map/all_to_all | solution.py:51
  174.7 7.4 %shard_map.137 = (f32[64,8,128]{2,1,0:T(8,128)}, f32[3,3584]{1,0:T(4,128)}) custom-call(f32[8,24,128]{2,1,0:T(8,128)} %all_to_all.80.full_ref, f32[8,24,128]{2,1,0:T(8,128)} %bitcast.9, f32[64,8,128]{2,1,0:T(8,128)} %all_to_all.78.recv_ref, s32[1,3584]{1,0:T(1,128)} %broadcast_in_dim.25.ia_ref, f32[18,3584]{1,0:T(8,128)} %ja_ref.9), custom_call_target="tpu_custom_call" | custom-call | tf_op jit(solution)/shard_map/pallas_call | solution.py:344
  182.0 18.3 %all_to_all.81.ret_ref = f32[64,8,128]{2,1,0:T(8,128)} all-to-all(f32[64,8,128]{2,1,0:T(8,128)} %get-tuple-element.21), channel_id=1, replica_groups=mesh['contact_0'=4,'contact_1'=2,'body'=8,'group'=8] {'body','group'}, dimensions={0} | all-to-all | bytes 524288 | tf_op jit(solution)/shard_map/all_to_all | solution.py:51
  203.1 10.0 %all_to_all.82 = f32[8,8,128]{2,1,0:T(8,128)S(1)} all-to-all(f32[8,8,128]{2,1,0:T(8,128)S(1)} %broadcast_in_dim.33), channel_id=1, replica_groups=mesh['contact_0'=4,'contact_1'=2,'body'=8,'group'=8] {'contact_0','conta..., dimensions={0} | all-to-all | bytes 65536 | tf_op jit(solution)/shard_map/all_to_all | solution.py:51
  213.2 17.5 %all_to_all.83.refs_1_ = f32[64,8,128]{2,1,0:T(8,128)} all-to-all(f32[64,8,128]{2,1,0:T(8,128)S(1)} %broadcast_in_dim.34), channel_id=1, replica_groups=mesh['contact_0'=4,'contact_1'=2,'body'=8,'group'=8] {'body','group'}, dimensions={0} | all-to-all | bytes 524288 | tf_op jit(solution)/shard_map/all_to_all | solution.py:51
  230.7 2.5 shard_map.139
  233.2 18.1 %all_to_all.84.recv_ref = f32[64,8,128]{2,1,0:T(8,128)} all-to-all(f32[64,8,128]{2,1,0:T(8,128)} %get-tuple-element.27), channel_id=1, replica_groups=mesh['contact_0'=4,'contact_1'=2,'body'=8,'group'=8] {'body','group'}, dimensions={0} | all-to-all | bytes 524288 | tf_op jit(solution)/shard_map/all_to_all | solution.py:51
  251.3 8.0 %shard_map.140 = f32[8,24,128]{2,1,0:T(8,128)} custom-call(f32[64,8,128]{2,1,0:T(8,128)} %all_to_all.84.recv_ref, f32[18,3584]{1,0:T(8,128)} %ja_ref.9, f32[3,3584]{1,0:T(4,128)} %get-tuple-element.13.y_ref, s32[1,3584]{1,0:T(1,128)} %broadcast_in_dim.25.ia_ref), custom_call_target="tpu_custom_call" | custom-call | tf_op jit(solution)/shard_map/pallas_call | solution.py:331
  259.3 12.1 %all_to_all.85 = f32[8,24,128]{2,1,0:T(8,128)S(1)} all-to-all(f32[8,24,128]{2,1,0:T(8,128)} %shard_map.140), channel_id=1, replica_groups=mesh['contact_0'=4,'contact_1'=2,'body'=8,'group'=8] {'contact_0','conta..., dimensions={0} | all-to-all | bytes 196608 | tf_op jit(solution)/shard_map/all_to_all | solution.py:51
  271.4 8.2 %all_to_all.86 = f32[8,24,128]{2,1,0:T(8,128)S(1)} all-to-all(f32[8,24,128]{2,1,0:T(8,128)S(1)} %broadcast_in_dim.70), channel_id=1, replica_groups=mesh['contact_0'=4,'contact_1'=2,'body'=8,'group'=8] {'contact_0','conta..., dimensions={0} | all-to-all | bytes 196608 | tf_op jit(solution)/shard_map/all_to_all | solution.py:51
  (46 shorter events, 21.2 us)
Async XLA Ops:
  0.6 0.7 copy-start.8
  5.4 17.3 %copy-start.5 = (s32[3584]{0:T(1024)S(1)}, s32[3584]{0:T(1024)}, u32[]{:S(2)}) copy-start(s32[3584]{0:T(1024)} %param.19) | copy-start | bytes 43012
  5.4 29.9 %all-to-all-start = ((f32[64,8,128]{2,1,0:T(8,128)}), f32[64,8,128]{2,1,0:T(8,128)S(1)}, u32[]{:S(2)}, u32[]{:S(2)}) async-start(f32[64,8,128]{2,1,0:T(8,128)} %shard_map.131), calls=%async_computation | async-start | bytes 524288 | tf_op jit(solution)/shard_map/all_to_all | solution.py:51
  35.3 0.7 copy-start
  56.5 4.7 %copy-start.2 = (f32[6,4096]{1,0:T(8,128)S(1)}, f32[6,4096]{1,0:T(8,128)}, u32[]{:S(2)}) copy-start(f32[6,4096]{1,0:T(8,128)} %param.22) | copy-start | bytes 294916
  57.1 9.1 %all-to-all-start.2 = ((f32[8,24,128]{2,1,0:T(8,128)}), f32[8,24,128]{2,1,0:T(8,128)S(1)}, u32[]{:S(2)}, u32[]{:S(2)}) async-start(f32[8,24,128]{2,1,0:T(8,128)} %broadcast_in_dim.26), calls=%async_computation.2 | async-start | bytes 196608 | tf_op jit(solution)/shard_map/all_to_all | solution.py:51
  66.2 0.6 copy-start.3
  106.7 4.8 %copy-start.6 = (f32[3584]{0:T(1024)S(1)}, f32[3584]{0:T(1024)}, u32[]{:S(2)}) copy-start(f32[3584]{0:T(1024)} %param.17) | copy-start | bytes 43012
  106.7 17.7 %all-to-all-start.5 = ((f32[64,8,128]{2,1,0:T(8,128)}), f32[64,8,128]{2,1,0:T(8,128)S(1)}, u32[]{:S(2)}, u32[]{:S(2)}) async-start(f32[64,8,128]{2,1,0:T(8,128)} %broadcast_in_dim.29), calls=%async_computation.5 | async-start | bytes 524288 | tf_op jit(solution)/shard_map/all_to_all | solution.py:51
  111.4 0.7 copy-start.7
  124.4 0.7 copy-start.1
  279.6 0.9 copy-start.4

commit v2 on v1

--- a/solution.py
+++ b/solution.py
@@ -45,10 +45,6 @@
     earlier = (ordinal[None, :] < ordinal[:, None]).astype(jnp.int32)
     ranking = jnp.sum(matching * earlier, axis=1)
     return target * capacity + ranking
-
-
-def exchange(array, axes):
-    return lax.all_to_all(array, axes, 0, 0, tiled=True)
 
 
 def impulse_rows(jacobian, values):
@@ -238,8 +234,7 @@
     momentum, places_ref, sums_ref, y_ref, g_ref, xp_ref, mu_ref, act_ref, jb_ref, ib_ref,
     x_ref, yn_ref, out_ref,
 ):
-    total = jnp.sum(sums_ref[...], axis=0)
-    total = jnp.sum(total, axis=1, keepdims=True)
+    total = jnp.sum(sums_ref[...], axis=1, keepdims=True)
     stride = jnp.sqrt((total[0:1] + EPS) / (total[1:2] + EPS))
     z = y_ref[...] - stride * g_ref[...]
     mu = mu_ref[...]
@@ -261,6 +256,156 @@
     following = projected + momentum * (projected - xp_ref[...])
     yn_ref[...] = following
     pack_rows(places_ref, packed_terms(jb_ref[...], following, ib_ref[...]), out_ref)
+
+
+def remote(src, dst, send_sem, recv_sem, device_id):
+    return pltpu.make_async_remote_copy(
+        src_ref=src,
+        dst_ref=dst,
+        send_sem=send_sem,
+        recv_sem=recv_sem,
+        device_id=device_id,
+        device_id_type=pl.DeviceIdType.MESH,
+    )
+
+
+def contact_id(index):
+    return {"contact_0": index // 2, "contact_1": lax.rem(index, 2)}
+
+
+def greet(ids):
+    barrier = pltpu.get_barrier_semaphore()
+    for device_id in ids:
+        pl.semaphore_signal(
+            barrier, inc=1, device_id=device_id, device_id_type=pl.DeviceIdType.MESH
+        )
+    pl.semaphore_wait(barrier, len(ids))
+
+
+def trade_kernel(src_ref, dst_ref, send_sem, recv_sem):
+    body, group = lax.axis_index("body"), lax.axis_index("group")
+    bodies, groups = lax.axis_size("body"), lax.axis_size("group")
+    me = body * groups + group
+
+    def to(k):
+        return lax.rem(body + k // groups, bodies), lax.rem(group + lax.rem(k, groups), groups)
+
+    def source(k):
+        b = lax.rem(body - k // groups + bodies, bodies)
+        return b * groups + lax.rem(group - lax.rem(k, groups) + groups, groups)
+
+    def signal(k, carry):
+        b, g = to(k)
+        pl.semaphore_signal(
+            pltpu.get_barrier_semaphore(),
+            inc=1,
+            device_id={"body": b, "group": g},
+            device_id_type=pl.DeviceIdType.MESH,
+        )
+        return carry
+
+    lax.fori_loop(1, bodies * groups, signal, 0)
+    pl.semaphore_wait(pltpu.get_barrier_semaphore(), bodies * groups - 1)
+
+    def send(k, carry):
+        b, g = to(k)
+        remote(
+            src_ref.at[b * groups + g],
+            dst_ref.at[me],
+            send_sem.at[k],
+            recv_sem.at[k],
+            {"body": b, "group": g},
+        ).start()
+        return carry
+
+    lax.fori_loop(1, bodies * groups, send, 0)
+    dst_ref[me] = src_ref[me]
+
+    def wait(k, carry):
+        b, g = to(k)
+        copy = remote(
+            src_ref.at[b * groups + g],
+            dst_ref.at[source(k)],
+            send_sem.at[k],
+            recv_sem.at[k],
+            {"body": b, "group": g},
+        )
+        copy.wait_send()
+        copy.wait_recv()
+        return carry
+
+    lax.fori_loop(1, bodies * groups, wait, 0)
+
+
+def contact_kernel(part_ref, full_ref, land_ref, mine_ref, send_sem, recv_sem):
+    n = part_ref.shape[0]
+    me = lax.axis_index("contact_0") * 2 + lax.axis_index("contact_1")
+    peers = [lax.rem(me + k, n) for k in range(1, n)]
+    greet([contact_id(p) for p in peers])
+    copies = []
+    for k, p in enumerate(peers):
+        copy = remote(
+            part_ref.at[p], land_ref.at[k], send_sem.at[0, k], recv_sem.at[0, k], contact_id(p)
+        )
+        copy.start()
+        copies.append(copy)
+    total = part_ref[me]
+    for k, copy in enumerate(copies):
+        copy.wait_recv()
+        total = total + land_ref[k]
+    mine_ref[...] = total
+    full_ref[me] = total
+    for k, p in enumerate(peers):
+        copy = remote(
+            mine_ref, full_ref.at[me], send_sem.at[1, k], recv_sem.at[1, k], contact_id(p)
+        )
+        copy.start()
+        copies.append(copy)
+    for k in range(n - 1):
+        copies[k].wait_send()
+        copies[n - 1 + k].wait_send()
+        sender = lax.rem(me - (k + 1) + n, n)
+        remote(
+            mine_ref,
+            full_ref.at[sender],
+            send_sem.at[1, k],
+            recv_sem.at[1, k],
+            contact_id(peers[k]),
+        ).wait_recv()
+
+
+def sums_kernel(sums_ref, out_ref, land_ref, held_ref, send_sem, recv_sem):
+    n = land_ref.shape[1]
+    axes = (
+        (lax.axis_index("contact_0") * 2 + lax.axis_index("contact_1"), contact_id),
+        (lax.axis_index("body"), lambda p: {"body": p}),
+        (lax.axis_index("group"), lambda p: {"group": p}),
+    )
+    peers = [[lax.rem(me + k, n) for k in range(1, n)] for me, _ in axes]
+    greet([name(p) for (_, name), row in zip(axes, peers) for p in row])
+    for a, (me, name) in enumerate(axes):
+        src = sums_ref if a == 0 else held_ref.at[a - 1]
+        copies = []
+        for k, p in enumerate(peers[a]):
+            copy = remote(
+                src, land_ref.at[a, me], send_sem.at[a, k], recv_sem.at[a, k], name(p)
+            )
+            copy.start()
+            copies.append(copy)
+        land_ref[a, me] = src[...]
+        for k, p in enumerate(peers[a]):
+            copies[k].wait_send()
+            sender = lax.rem(me - (k + 1) + n, n)
+            remote(
+                src, land_ref.at[a, sender], send_sem.at[a, k], recv_sem.at[a, k], name(p)
+            ).wait_recv()
+        total = land_ref[a, 0]
+        for i in range(1, n):
+            total = total + land_ref[a, i]
+        if a < 2:
+            held_ref[a] = total
+        else:
+            out_ref[...] = total
 
 
 def f32(*shape):
@@ -327,10 +472,43 @@
         scratch_shapes=[pltpu.VMEM((8, count), jnp.float32)],
     )
 
+    def call(kernel, shape, scratch, number):
+        return pl.pallas_call(
+            kernel,
+            out_shape=shape,
+            in_specs=[VMEM],
+            out_specs=VMEM,
+            scratch_shapes=scratch,
+            compiler_params=pltpu.CompilerParams(collective_id=number, has_side_effects=True),
+        )
+
+    dma = pltpu.SemaphoreType.DMA
+    trade = call(trade_kernel, f32(shards, 8, 128), [dma((shards,)), dma((shards,))], 0)
+    share = call(
+        contact_kernel,
+        f32(sharers, 24, 128),
+        [
+            pltpu.VMEM((sharers - 1, 24, 128), jnp.float32),
+            pltpu.VMEM((24, 128), jnp.float32),
+            dma((2, sharers - 1)),
+            dma((2, sharers - 1)),
+        ],
+        1,
+    )
+    add_up = call(
+        sums_kernel,
+        f32(8, 128),
+        [
+            pltpu.VMEM((3, sharers, 8, 128), jnp.float32),
+            pltpu.VMEM((2, 8, 128), jnp.float32),
+            dma((3, sharers - 1)),
+            dma((3, sharers - 1)),
+        ],
+        2,
+    )
+
     def body_impulse(received, values):
-        partial = exchange(scatter(received, jacobian_a, values, index_a), CONTACT)
-        mine = jnp.sum(partial, axis=0)
-        return exchange(jnp.broadcast_to(mine[None], (sharers, *mine.shape)), CONTACT)
+        return share(scatter(received, jacobian_a, values, index_a))
 
     momentum = momentum_table(ITERS)
     current = warm_start
@@ -339,16 +517,14 @@
     latest = warm_start
     packed = pack(places, jacobian_b, warm_start, index_b)
     for rounds in range(ITERS):
-        received = exchange(packed, SHARD)
+        received = trade(packed)
         full = body_impulse(received, current)
         returned, near = gather(full, mass, received, index_a, jacobian_a)
         gradient, sums = gradient_call(
-            places, exchange(returned, SHARD), near, jacobian_b, compliance, free_gap,
+            places, trade(returned), near, jacobian_b, compliance, free_gap,
             current, before, gradient_before,
         )
-        sums = exchange(jnp.broadcast_to(sums[None], (sharers, 8, 128)), CONTACT)
-        sums = jnp.sum(sums, axis=0)
-        sums = exchange(jnp.broadcast_to(sums[None], (shards, 8, 128)), SHARD)
+        sums = add_up(sums)
         last = rounds == ITERS - 1
         step = pl.pallas_call(
             lambda *refs, m=0.0 if last else momentum[rounds]: step_kernel(m, *refs),
@@ -360,7 +536,7 @@
             places, sums, current, gradient, latest, mu, active, jacobian_b, index_b
         )
         before, gradient_before, latest, current = current, gradient, projected, following
-    full = body_impulse(exchange(packed, SHARD), latest)
+    full = body_impulse(trade(packed), latest)
     total = full.reshape(12, 2, 8, 128).transpose(0, 2, 1, 3).reshape(inverse_mass.shape)
     velocity = free_velocity + inverse_mass * total
     return (latest, velocity)

time: 283 us -> 240 us (0.85)
  Pallas kernels: 49.9 us -> 229 us
  blocking collectives: 164 us -> 0 us
  waiting for transfers between devices: 27.9 us -> 0 us
  starting transfers between devices: 26.1 us -> 0 us
  local copies, waits for them, and re-layouts: 11 us -> 8.14 us
    pallas_call x5 -> x15, Pallas kernels: 28.2 us -> 208 us  [the longest x6 67.9 us: body_impulse(): return share(scatter(received, jacobian_a, values, index_a))]
    all_to_all x12 -> x0, blocking collectives: 164 us -> none  [exchange(): return lax.all_to_all(array, axes, 0, 0, tiled=True)]
    all_to_all x3 -> x0, waiting for transfers between devices: 27.9 us -> none  [exchange(): return lax.all_to_all(array, axes, 0, 0, tiled=True)]
    all_to_all x3 -> x0, starting transfers between devices: 26.1 us -> none  [exchange(): return lax.all_to_all(array, axes, 0, 0, tiled=True)]
  transfers between devices with their start and end apart: 3 -> 0, of which waited for: 3 -> 0; matrix products, arithmetic and copies ran while one was open for 1% -> 0% of each run, Pallas kernels for 0% -> 0%
where the time goes in v2:
time: 240 us; the launch traced here: 239 us
  Pallas kernels  229 us (95%)
  local copies, waits for them, and re-layouts  8.14 us (3%)
    pallas_call x6, Pallas kernels, body_impulse(): return share(scatter(received, jacobian_a, values, index_a))  67.9 us
    pallas_call x2, Pallas kernels, on_device(): received = trade(packed)  44.9 us
    pallas_call x2, Pallas kernels, on_device(): trade(returned)  38.2 us
    pallas_call x2, Pallas kernels, on_device(): sums = add_up(sums)  34.7 us
    pallas_call x1, Pallas kernels, on_device(): full = body_impulse(trade(packed), latest)  17.5 us
    pallas_call x2, Pallas kernels, on_device(): returned, near = gather(full, mass, received, index_a, jacobian_a)  14.7 us

profile of v2, /device:TPU:1, one launch (start us, length us, event | category | flops | bytes accessed | tf_op | source)
XLA Modules:
  0.0 239.3 jit_solution(11890272113323845490)
XLA Ops:
  2.0 1.3 broadcast_in_dim.18.ia_ref
  5.4 1.0 reshape.17
  7.1 2.0 shard_map.131.src_ref
  9.0 27.3 %shard_map.132.recv_ref = f32[64,8,128]{2,1,0:T(8,128)} custom-call(f32[64,8,128]{2,1,0:T(8,128)} %shard_map.131.src_ref), custom_call_target="tpu_custom_call" | custom-call | tf_op jit(solution)/shard_map/pallas_call | solution.py:520
  36.3 8.0 %shard_map.133.part_ref = f32[8,24,128]{2,1,0:T(8,128)} custom-call(f32[64,8,128]{2,1,0:T(8,128)} %shard_map.132.recv_ref, f32[18,3584]{1,0:T(8,128)} %ja_ref.9, f32[3,3584]{1,0:T(4,128)} %yp_ref.1, s32[1,3584]{1,0:T(1,128)} %broadcast_in_dim.18.ia_ref), custom_call_target="tpu_custom_call" | custom-call | tf_op jit(solution)/shard_map/pallas_call | solution.py:511
  44.3 14.7 %shard_map.134.full_ref = f32[8,24,128]{2,1,0:T(8,128)} custom-call(f32[8,24,128]{2,1,0:T(8,128)} %shard_map.133.part_ref), custom_call_target="tpu_custom_call" | custom-call | tf_op jit(solution)/shard_map/pallas_call | solution.py:511
  59.0 7.3 %shard_map.135 = (f32[64,8,128]{2,1,0:T(8,128)}, f32[3,3584]{1,0:T(4,128)}) custom-call(f32[8,24,128]{2,1,0:T(8,128)} %shard_map.134.full_ref, f32[8,24,128]{2,1,0:T(8,128)} %bitcast.8, f32[64,8,128]{2,1,0:T(8,128)} %shard_map.132.recv_ref, s32[1,3584]{1,0:T(1,128)} %broadcast_in_dim.18.ia_ref, f32[18,3584]{1,0:T(8,128)} %ja_ref.9), custom_call_target="tpu_custom_call" | custom-call | tf_op jit(solution)/shard_map/pallas_call | solution.py:522
  66.3 19.3 %shard_map.136.ret_ref = f32[64,8,128]{2,1,0:T(8,128)} custom-call(f32[64,8,128]{2,1,0:T(8,128)} %get-tuple-element.15.src_ref), custom_call_target="tpu_custom_call" | custom-call | tf_op jit(solution)/shard_map/pallas_call | solution.py:524
  86.3 2.1 shard_map.137
  88.4 17.8 %shard_map.138.refs_1_ = f32[8,128]{1,0:T(8,128)} custom-call(f32[8,128]{1,0:T(8,128)} %get-tuple-element.17.sums_ref), custom_call_target="tpu_custom_call" | custom-call | tf_op jit(solution)/shard_map/pallas_call | solution.py:527
  106.2 2.4 shard_map.139
  108.6 17.6 %shard_map.140.recv_ref = f32[64,8,128]{2,1,0:T(8,128)} custom-call(f32[64,8,128]{2,1,0:T(8,128)} %get-tuple-element.19.src_ref), custom_call_target="tpu_custom_call" | custom-call | tf_op jit(solution)/shard_map/pallas_call | solution.py:520
  126.2 8.0 %shard_map.141.part_ref = f32[8,24,128]{2,1,0:T(8,128)} custom-call(f32[64,8,128]{2,1,0:T(8,128)} %shard_map.140.recv_ref, f32[18,3584]{1,0:T(8,128)} %ja_ref.9, f32[3,3584]{1,0:T(4,128)} %get-tuple-element.20.y_ref.refs_2_, s32[1,3584]{1,0:T(1,128)} %broadcast_in_dim.18.ia_ref), custom_call_target="tpu_custom_call" | custom-call | tf_op jit(solution)/shard_map/pallas_call | solution.py:511
  134.2 14.8 %shard_map.142.full_ref = f32[8,24,128]{2,1,0:T(8,128)} custom-call(f32[8,24,128]{2,1,0:T(8,128)} %shard_map.141.part_ref), custom_call_target="tpu_custom_call" | custom-call | tf_op jit(solution)/shard_map/pallas_call | solution.py:511
  149.0 7.3 %shard_map.143 = (f32[64,8,128]{2,1,0:T(8,128)}, f32[3,3584]{1,0:T(4,128)}) custom-call(f32[8,24,128]{2,1,0:T(8,128)} %shard_map.142.full_ref, f32[8,24,128]{2,1,0:T(8,128)} %bitcast.9, f32[64,8,128]{2,1,0:T(8,128)} %shard_map.140.recv_ref, s32[1,3584]{1,0:T(1,128)} %broadcast_in_dim.18.ia_ref, f32[18,3584]{1,0:T(8,128)} %ja_ref.9), custom_call_target="tpu_custom_call" | custom-call | tf_op jit(solution)/shard_map/pallas_call | solution.py:522
  156.4 18.9 %shard_map.144.ret_ref = f32[64,8,128]{2,1,0:T(8,128)} custom-call(f32[64,8,128]{2,1,0:T(8,128)} %get-tuple-element.21.src_ref), custom_call_target="tpu_custom_call" | custom-call | tf_op jit(solution)/shard_map/pallas_call | solution.py:524
  175.3 2.1 shard_map.145
  177.4 16.9 %shard_map.146.refs_1_ = f32[8,128]{1,0:T(8,128)} custom-call(f32[8,128]{1,0:T(8,128)} %get-tuple-element.23.sums_ref), custom_call_target="tpu_custom_call" | custom-call | tf_op jit(solution)/shard_map/pallas_call | solution.py:527
  194.4 2.4 shard_map.147
  196.7 17.5 %shard_map.148.recv_ref = f32[64,8,128]{2,1,0:T(8,128)} custom-call(f32[64,8,128]{2,1,0:T(8,128)} %get-tuple-element.27.src_ref), custom_call_target="tpu_custom_call" | custom-call | tf_op jit(solution)/shard_map/pallas_call | solution.py:539
  214.3 8.0 %shard_map.149.part_ref = f32[8,24,128]{2,1,0:T(8,128)} custom-call(f32[64,8,128]{2,1,0:T(8,128)} %shard_map.148.recv_ref, f32[18,3584]{1,0:T(8,128)} %ja_ref.9, f32[3,3584]{1,0:T(4,128)} %get-tuple-element.13.y_ref, s32[1,3584]{1,0:T(1,128)} %broadcast_in_dim.18.ia_ref), custom_call_target="tpu_custom_call" | custom-call | tf_op jit(solution)/shard_map/pallas_call | solution.py:511
  222.3 14.5 %shard_map.150 = f32[8,24,128]{2,1,0:T(8,128)} custom-call(f32[8,24,128]{2,1,0:T(8,128)} %shard_map.149.part_ref), custom_call_target="tpu_custom_call" | custom-call | tf_op jit(solution)/shard_map/pallas_call | solution.py:511
  236.8 1.0 copy.17
  237.8 0.8 copy-done
  (20 shorter events, 5.5 us)
Async XLA Ops:
  0.6 0.7 copy-start.5
  1.5 1.9 copy-start.2
  3.4 0.7 copy-start.3
  4.1 0.7 copy-start.4
  236.7 1.1 copy-start.1
  237.7 0.9 copy-start

commit v3 on v2

--- a/solution.py
+++ b/solution.py
@@ -1,3 +1,4 @@
+import functools
 import math
 
 import jax
@@ -141,66 +142,6 @@
 
 def pack_kernel(places_ref, jb_ref, y_ref, ib_ref, out_ref):
     pack_rows(places_ref, packed_terms(jb_ref[...], y_ref[...], ib_ref[...]), out_ref)
-
-
-def scatter_kernel(recv_ref, ja_ref, y_ref, ia_ref, out_ref, near_ref, acc_ref):
-    near_ref[...] = impulse_rows(ja_ref[...], y_ref[...])
-    acc_ref[...] = jnp.zeros_like(acc_ref)
-
-    def far(i, carry):
-        tiles = [recv_ref[WIDE * i + k] for k in range(WIDE)]
-        both = jnp.concatenate(tiles, axis=1)
-        scatter_chunk(acc_ref, both[0:6], both[6:7].astype(jnp.int32))
-        return carry
-
-    lax.fori_loop(0, recv_ref.shape[0] // WIDE, far, 0)
-
-    def near(i, carry):
-        at = pl.ds(pl.multiple_of(i * CHUNK, CHUNK), CHUNK)
-        scatter_chunk(acc_ref, near_ref[:, at], ia_ref[:, at])
-        return carry
-
-    lax.fori_loop(0, ia_ref.shape[1] // CHUNK, near, 0)
-    for t in range(24):
-        g, half = t // 2, t % 2
-        at = slice(128 * half, 128 * half + 128)
-        out_ref[t // 3, 8 * (t % 3) : 8 * (t % 3) + 8, :] = (
-            acc_ref[8 * g : 8 * g + 8, at] + acc_ref[96 + 8 * g : 104 + 8 * g, at]
-        )
-
-
-def gather_kernel(full_ref, mass_ref, recv_ref, ia_ref, ja_ref, ret_ref, near_ref, tab_ref, va_ref):
-    groups = []
-    for g in range(12):
-        halves = []
-        for half in range(2):
-            t = 2 * g + half
-            at = slice(8 * (t % 3), 8 * (t % 3) + 8)
-            halves.append(full_ref[t // 3, at, :] * mass_ref[t // 3, at, :])
-        groups.append(jnp.concatenate(halves, axis=1))
-    velocities = jnp.concatenate(groups, axis=0)
-    high, low = pair(velocities)
-    tab_ref[...] = jnp.concatenate([high, low], axis=0).astype(jnp.bfloat16)
-    pad = jnp.zeros((2, CHUNK), jnp.float32)
-
-    def far(i, carry):
-        tiles = [recv_ref[WIDE * i + k, 6:7, :] for k in range(WIDE)]
-        index = jnp.concatenate(tiles, axis=1).astype(jnp.int32)
-        rows = jnp.concatenate(gather_chunk(tab_ref[...], index) + [pad], axis=0)
-        for k in range(WIDE):
-            ret_ref[WIDE * i + k] = rows[:, 128 * k : 128 * (k + 1)]
-        return carry
-
-    lax.fori_loop(0, recv_ref.shape[0] // WIDE, far, 0)
-
-    def near(i, carry):
-        at = pl.ds(pl.multiple_of(i * CHUNK, CHUNK), CHUNK)
-        rows = gather_chunk(tab_ref[...], ia_ref[:, at]) + [pad]
-        va_ref[:, at] = jnp.concatenate(rows, axis=0)
-        return carry
-
-    lax.fori_loop(0, ia_ref.shape[1] // CHUNK, near, 0)
-    near_ref[...] = velocity_rows(ja_ref[...], va_ref[0:6, :])
 
 
 def gradient_kernel(
@@ -273,105 +214,178 @@
     return {"contact_0": index // 2, "contact_1": lax.rem(index, 2)}
 
 
-def greet(ids):
-    barrier = pltpu.get_barrier_semaphore()
-    for device_id in ids:
-        pl.semaphore_signal(
-            barrier, inc=1, device_id=device_id, device_id_type=pl.DeviceIdType.MESH
-        )
-    pl.semaphore_wait(barrier, len(ids))
-
-
-def trade_kernel(src_ref, dst_ref, send_sem, recv_sem):
+def signal(device_id):
+    pl.semaphore_signal(
+        pltpu.get_barrier_semaphore(),
+        inc=1,
+        device_id=device_id,
+        device_id_type=pl.DeviceIdType.MESH,
+    )
+
+
+def middle_kernel(final, packed_ref, mass_ref, ja_ref, y_ref, ia_ref, *refs):
+    outs = 1 if final else 2
+    (recv_ref, near_ref, acc_ref, part_ref, land_ref, mine_ref, go_send, go_recv, c_send, c_recv) = (
+        refs[outs : outs + 10]
+    )
+    if final:
+        full_ref = refs[0]
+    else:
+        ret_ref, nearv_ref = refs[:2]
+        full_ref, back_ref, tab_ref, va_ref, back_send, back_recv = refs[outs + 10 :]
     body, group = lax.axis_index("body"), lax.axis_index("group")
     bodies, groups = lax.axis_size("body"), lax.axis_size("group")
+    shards = bodies * groups
     me = body * groups + group
+    n = part_ref.shape[0]
+    mine = lax.axis_index("contact_0") * 2 + lax.axis_index("contact_1")
+    peers = [lax.rem(mine + k, n) for k in range(1, n)]
 
     def to(k):
         return lax.rem(body + k // groups, bodies), lax.rem(group + lax.rem(k, groups), groups)
 
     def source(k):
         b = lax.rem(body - k // groups + bodies, bodies)
-        return b * groups + lax.rem(group - lax.rem(k, groups) + groups, groups)
-
-    def signal(k, carry):
+        return b, lax.rem(group - lax.rem(k, groups) + groups, groups)
+
+    def name(b, g):
+        return {"body": b, "group": g}
+
+    def going(k):
         b, g = to(k)
-        pl.semaphore_signal(
-            pltpu.get_barrier_semaphore(),
-            inc=1,
-            device_id={"body": b, "group": g},
-            device_id_type=pl.DeviceIdType.MESH,
-        )
-        return carry
-
-    lax.fori_loop(1, bodies * groups, signal, 0)
-    pl.semaphore_wait(pltpu.get_barrier_semaphore(), bodies * groups - 1)
-
-    def send(k, carry):
-        b, g = to(k)
-        remote(
-            src_ref.at[b * groups + g],
-            dst_ref.at[me],
-            send_sem.at[k],
-            recv_sem.at[k],
-            {"body": b, "group": g},
-        ).start()
-        return carry
-
-    lax.fori_loop(1, bodies * groups, send, 0)
-    dst_ref[me] = src_ref[me]
-
-    def wait(k, carry):
-        b, g = to(k)
-        copy = remote(
-            src_ref.at[b * groups + g],
-            dst_ref.at[source(k)],
-            send_sem.at[k],
-            recv_sem.at[k],
-            {"body": b, "group": g},
-        )
-        copy.wait_send()
-        copy.wait_recv()
-        return carry
-
-    lax.fori_loop(1, bodies * groups, wait, 0)
-
-
-def contact_kernel(part_ref, full_ref, land_ref, mine_ref, send_sem, recv_sem):
-    n = part_ref.shape[0]
-    me = lax.axis_index("contact_0") * 2 + lax.axis_index("contact_1")
-    peers = [lax.rem(me + k, n) for k in range(1, n)]
-    greet([contact_id(p) for p in peers])
+        at = b * groups + g
+        return remote(packed_ref.at[at], recv_ref.at[k], go_send.at[k], go_recv.at[k], name(b, g))
+
+    def backing(k):
+        b, g = source(k)
+        return remote(back_ref.at[k], ret_ref.at[me], back_send.at[k], back_recv.at[k], name(b, g))
+
+    def loop(low, high, act):
+        def turn(k, carry):
+            act(k)
+            return carry
+
+        lax.fori_loop(low, high, turn, 0)
+
+    loop(1, shards, lambda k: signal(name(*to(k))))
+    for p in peers:
+        signal(contact_id(p))
+
+    near_ref[...] = impulse_rows(ja_ref[...], y_ref[...])
+    acc_ref[...] = jnp.zeros_like(acc_ref)
+
+    def near(i):
+        at = pl.ds(pl.multiple_of(i * CHUNK, CHUNK), CHUNK)
+        scatter_chunk(acc_ref, near_ref[:, at], ia_ref[:, at])
+
+    loop(0, ia_ref.shape[1] // CHUNK, near)
+    pl.semaphore_wait(pltpu.get_barrier_semaphore(), shards - 1 + n - 1)
+
+    loop(1, shards, lambda k: going(k).start())
+    recv_ref[0] = packed_ref[me]
+
+    def far(i, first=0):
+        for k in range(first, WIDE):
+            going(WIDE * i + k).wait_recv()
+        both = jnp.concatenate([recv_ref[WIDE * i + k] for k in range(WIDE)], axis=1)
+        scatter_chunk(acc_ref, both[0:6], both[6:7].astype(jnp.int32))
+
+    far(0, 1)
+    loop(1, shards // WIDE, far)
+
+    for t in range(24):
+        g, half = t // 2, t % 2
+        at = slice(128 * half, 128 * half + 128)
+        part_ref[t // 3, 8 * (t % 3) : 8 * (t % 3) + 8, :] = (
+            acc_ref[8 * g : 8 * g + 8, at] + acc_ref[96 + 8 * g : 104 + 8 * g, at]
+        )
+    loop(1, shards, lambda k: going(k).wait_send())
     copies = []
     for k, p in enumerate(peers):
         copy = remote(
-            part_ref.at[p], land_ref.at[k], send_sem.at[0, k], recv_sem.at[0, k], contact_id(p)
+            part_ref.at[p], land_ref.at[k], c_send.at[0, k], c_recv.at[0, k], contact_id(p)
         )
         copy.start()
         copies.append(copy)
-    total = part_ref[me]
+    total = part_ref[mine]
     for k, copy in enumerate(copies):
         copy.wait_recv()
         total = total + land_ref[k]
     mine_ref[...] = total
-    full_ref[me] = total
+    full_ref[mine] = total
     for k, p in enumerate(peers):
         copy = remote(
-            mine_ref, full_ref.at[me], send_sem.at[1, k], recv_sem.at[1, k], contact_id(p)
+            mine_ref, full_ref.at[mine], c_send.at[1, k], c_recv.at[1, k], contact_id(p)
         )
         copy.start()
         copies.append(copy)
     for k in range(n - 1):
         copies[k].wait_send()
         copies[n - 1 + k].wait_send()
-        sender = lax.rem(me - (k + 1) + n, n)
+        sender = lax.rem(mine - (k + 1) + n, n)
         remote(
             mine_ref,
             full_ref.at[sender],
-            send_sem.at[1, k],
-            recv_sem.at[1, k],
+            c_send.at[1, k],
+            c_recv.at[1, k],
             contact_id(peers[k]),
         ).wait_recv()
+    if final:
+        return
+
+    rows = []
+    for g in range(12):
+        halves = []
+        for t in (2 * g, 2 * g + 1):
+            at = slice(8 * (t % 3), 8 * (t % 3) + 8)
+            halves.append(full_ref[t // 3, at, :] * mass_ref[t // 3, at, :])
+        rows.append(jnp.concatenate(halves, axis=1))
+    high, low = pair(jnp.concatenate(rows, axis=0))
+    tab_ref[...] = jnp.concatenate([high, low], axis=0).astype(jnp.bfloat16)
+    pad = jnp.zeros((2, CHUNK), jnp.float32)
+
+    def find(i):
+        tiles = [recv_ref[WIDE * i + k, 6:7, :] for k in range(WIDE)]
+        index = jnp.concatenate(tiles, axis=1).astype(jnp.int32)
+        found = jnp.concatenate(gather_chunk(tab_ref[...], index) + [pad], axis=0)
+        for k in range(WIDE):
+            back_ref[WIDE * i + k] = found[:, 128 * k : 128 * (k + 1)]
+
+    def give(i, first=0):
+        for k in range(first, WIDE):
+            backing(WIDE * i + k).start()
+
+    find(0)
+    find(1)
+    give(0, 1)
+
+    def find_give(i):
+        find(i)
+        give(i - 1)
+
+    loop(2, shards // WIDE, find_give)
+    ret_ref[me] = back_ref[0]
+    give(shards // WIDE - 1)
+
+    def near_find(i):
+        at = pl.ds(pl.multiple_of(i * CHUNK, CHUNK), CHUNK)
+        va_ref[:, at] = jnp.concatenate(gather_chunk(tab_ref[...], ia_ref[:, at]) + [pad], axis=0)
+
+    loop(0, ia_ref.shape[1] // CHUNK, near_find)
+    nearv_ref[...] = velocity_rows(ja_ref[...], va_ref[0:6, :])
+
+    def finish(k):
+        backing(k).wait_send()
+        b, g = to(k)
+        remote(
+            back_ref.at[k],
+            ret_ref.at[b * groups + g],
+            back_send.at[k],
+            back_recv.at[k],
+            name(b, g),
+        ).wait_recv()
+
+    loop(1, shards, finish)
 
 
 def sums_kernel(sums_ref, out_ref, land_ref, held_ref, send_sem, recv_sem):
@@ -382,7 +396,10 @@
         (lax.axis_index("group"), lambda p: {"group": p}),
     )
     peers = [[lax.rem(me + k, n) for k in range(1, n)] for me, _ in axes]
-    greet([name(p) for (_, name), row in zip(axes, peers) for p in row])
+    for (_, name), row in zip(axes, peers):
+        for p in row:
+            signal(name(p))
+    pl.semaphore_wait(pltpu.get_barrier_semaphore(), 3 * (n - 1))
     for a, (me, name) in enumerate(axes):
         src = sums_ref if a == 0 else held_ref.at[a - 1]
         copies = []
@@ -444,26 +461,6 @@
         in_specs=[SMEM, VMEM, VMEM, VMEM],
         out_specs=VMEM,
     )
-    scatter = pl.pallas_call(
-        scatter_kernel,
-        out_shape=f32(sharers, 24, 128),
-        in_specs=[VMEM] * 4,
-        out_specs=VMEM,
-        scratch_shapes=[
-            pltpu.VMEM((6, count), jnp.float32),
-            pltpu.VMEM((12 * ROWS, LANES), jnp.float32),
-        ],
-    )
-    gather = pl.pallas_call(
-        gather_kernel,
-        out_shape=(f32(shards, 8, 128), f32(3, count)),
-        in_specs=[VMEM] * 5,
-        out_specs=(VMEM, VMEM),
-        scratch_shapes=[
-            pltpu.VMEM((12 * ROWS, LANES), jnp.bfloat16),
-            pltpu.VMEM((8, count), jnp.float32),
-        ],
-    )
     gradient_call = pl.pallas_call(
         gradient_kernel,
         out_shape=(f32(3, count), f32(8, 128)),
@@ -472,43 +469,63 @@
         scratch_shapes=[pltpu.VMEM((8, count), jnp.float32)],
     )
 
-    def call(kernel, shape, scratch, number):
+    dma = pltpu.SemaphoreType.DMA
+
+    def call(kernel, operands, shape, scratch, number):
         return pl.pallas_call(
             kernel,
             out_shape=shape,
-            in_specs=[VMEM],
-            out_specs=VMEM,
+            in_specs=[VMEM] * operands,
+            out_specs=jax.tree.map(lambda _: VMEM, shape),
             scratch_shapes=scratch,
             compiler_params=pltpu.CompilerParams(collective_id=number, has_side_effects=True),
         )
 
-    dma = pltpu.SemaphoreType.DMA
-    trade = call(trade_kernel, f32(shards, 8, 128), [dma((shards,)), dma((shards,))], 0)
-    share = call(
-        contact_kernel,
-        f32(sharers, 24, 128),
-        [
-            pltpu.VMEM((sharers - 1, 24, 128), jnp.float32),
-            pltpu.VMEM((24, 128), jnp.float32),
-            dma((2, sharers - 1)),
-            dma((2, sharers - 1)),
+    def space(*shape):
+        return pltpu.VMEM(shape, jnp.float32)
+
+    common = [
+        space(shards, 8, 128),
+        space(6, count),
+        space(12 * ROWS, LANES),
+        space(sharers, 24, 128),
+        space(sharers - 1, 24, 128),
+        space(24, 128),
+        dma((shards,)),
+        dma((shards,)),
+        dma((2, sharers - 1)),
+        dma((2, sharers - 1)),
+    ]
+    middle = call(
+        functools.partial(middle_kernel, False),
+        5,
+        (f32(shards, 8, 128), f32(3, count)),
+        common
+        + [
+            space(sharers, 24, 128),
+            space(shards, 8, 128),
+            pltpu.VMEM((12 * ROWS, LANES), jnp.bfloat16),
+            space(8, count),
+            dma((shards,)),
+            dma((shards,)),
         ],
-        1,
+        0,
+    )
+    ending = call(
+        functools.partial(middle_kernel, True), 5, f32(sharers, 24, 128), common, 1
     )
     add_up = call(
         sums_kernel,
+        1,
         f32(8, 128),
         [
-            pltpu.VMEM((3, sharers, 8, 128), jnp.float32),
-            pltpu.VMEM((2, 8, 128), jnp.float32),
+            space(3, sharers, 8, 128),
+            space(2, 8, 128),
             dma((3, sharers - 1)),
             dma((3, sharers - 1)),
         ],
         2,
     )
-
-    def body_impulse(received, values):
-        return share(scatter(received, jacobian_a, values, index_a))
 
     momentum = momentum_table(ITERS)
     current = warm_start
@@ -517,11 +534,9 @@
     latest = warm_start
     packed = pack(places, jacobian_b, warm_start, index_b)
     for rounds in range(ITERS):
-        received = trade(packed)
-        full = body_impulse(received, current)
-        returned, near = gather(full, mass, received, index_a, jacobian_a)
+        returned, near = middle(packed, mass, jacobian_a, current, index_a)
         gradient, sums = gradient_call(
-            places, trade(returned), near, jacobian_b, compliance, free_gap,
+            places, returned, near, jacobian_b, compliance, free_gap,
             current, before, gradient_before,
         )
         sums = add_up(sums)
@@ -536,7 +551,7 @@
             places, sums, current, gradient, latest, mu, active, jacobian_b, index_b
         )
         before, gradient_before, latest, current = current, gradient, projected, following
-    full = body_impulse(trade(packed), latest)
+    full = ending(packed, mass, jacobian_a, latest, index_a)
     total = full.reshape(12, 2, 8, 128).transpose(0, 2, 1, 3).reshape(inverse_mass.shape)
     velocity = free_velocity + inverse_mass * total
     return (latest, velocity)

time: 240 us -> 182 us (0.76)
  Pallas kernels: 229 us -> 171 us
    pallas_call x15 -> x5, Pallas kernels: 187 us -> 129 us  [the longest x2 95.3 us: on_device(): returned, near = middle(packed, mass, jacobian_a, current, index_a)]
where the time goes in v3:
time: 182 us
  Pallas kernels  171 us (94%)
  local copies, waits for them, and re-layouts  8.16 us (4%)
    pallas_call x2, Pallas kernels, on_device(): returned, near = middle(packed, mass, jacobian_a, current, index_a)  95.3 us
    pallas_call x2, Pallas kernels, on_device(): sums = add_up(sums)  35.2 us
    pallas_call x1, Pallas kernels, on_device(): full = ending(packed, mass, jacobian_a, latest, index_a)  30 us
    pallas_call x2, Pallas kernels, on_device(): step(places, sums, current, gradient, latest, mu, active, jacobian_b, ind...  4.76 us
    pallas_call x2, Pallas kernels, on_device(): gradient_call(places, returned, near, jacobian_b, compliance, free_gap, c...  4.24 us

profile of v3, /device:TPU:1, one launch (start us, length us, event | category | flops | bytes accessed | tf_op | source)
XLA Modules:
  0.0 181.7 jit_solution(9372614090009642564)
XLA Ops:
  0.6 0.6 copy-done.5
  1.3 0.2 select_reduce_fusion
  1.5 0.5 multiply_add_fusion.1.places_ref.refs_0_
  2.0 1.3 broadcast_in_dim.18.ia_ref
  3.3 0.6 broadcast_in_dim.17.ib_ref.refs_8_
  4.1 0.6 broadcast_in_dim.20.refs_5_
  4.7 0.1 copy-done.4
  4.8 0.6 broadcast_in_dim.21.refs_6_
  5.4 1.0 reshape.17
  6.4 0.6 copy.16
  7.0 2.0 %shard_map.131.packed_ref = f32[64,8,128]{2,1,0:T(8,128)} custom-call(s32[56]{0:T(128)} %multiply_add_fusion.1.places_ref.refs_0_, f32[18,3584]{1,0:T(8,128)} %refs_7_.3, f32[3,3584]{1,0:T(4,128)} %yp_ref.1, s32[1,3584]{1,0:T(1,128)} %broadcast_in_dim.17.ib_ref.refs_8_), custom_call_target="tpu_custom_call" | custom-call | tf_op jit(solution)/shard_map/pallas_call | solution.py:535
  9.0 53.0 %shard_map.132 = (f32[64,8,128]{2,1,0:T(8,128)}, f32[3,3584]{1,0:T(4,128)}) custom-call(f32[64,8,128]{2,1,0:T(8,128)} %shard_map.131.packed_ref, f32[8,24,128]{2,1,0:T(8,128)} %bitcast.8, f32[18,3584]{1,0:T(8,128)} %ja_ref.5, f32[3,3584]{1,0:T(4,128)} %yp_ref.1, s32[1,3584]{1,0:T(1,128)} %broadcast_in_dim.18.ia_ref), custom_call_target="tpu_custom_call" | custom-call | tf_op jit(solution)/shard_map/pallas_call | solution.py:537
  62.0 0.6 broadcast_in_dim.19.yp_ref
  62.7 2.1 %shard_map.133 = (f32[3,3584]{1,0:T(4,128)}, f32[8,128]{1,0:T(8,128)}) custom-call(s32[56]{0:T(128)} %multiply_add_fusion.1.places_ref.refs_0_, f32[64,8,128]{2,1,0:T(8,128)} %get-tuple-element.15.ret_ref, f32[3,3584]{1,0:T(4,128)} %get-tuple-element.16.near_ref, f32[18,3584]{1,0:T(8,128)} %refs_7_.3, f32[3,3584]{1,0:T(4,128)} %comp_ref.3, ...), custom_call_target="tpu_custom_call" | custom-call | tf_op jit(solution)/shard_map/pallas_call | solution.py:538
  64.8 18.0 %shard_map.134.refs_1_ = f32[8,128]{1,0:T(8,128)} custom-call(f32[8,128]{1,0:T(8,128)} %get-tuple-element.17.sums_ref), custom_call_target="tpu_custom_call" | custom-call | tf_op jit(solution)/shard_map/pallas_call | solution.py:542
  82.8 2.4 %shard_map.135 = (f32[3,3584]{1,0:T(4,128)}, f32[3,3584]{1,0:T(4,128)}, f32[64,8,128]{2,1,0:T(8,128)}) custom-call(s32[56]{0:T(128)} %multiply_add_fusion.1.places_ref.refs_0_, f32[8,128]{1,0:T(8,128)} %shard_map.134.refs_1_, f32[3,3584]{1,0:T(4,128)} %yp_ref.1, f32[3,3584]{1,0:T(4,128)} %get-tuple-element.18.refs_3_.gp_ref, f32[3,3584]{1,0:T(4,128)} %yp_ref.1, ...), custom_call_target="tpu_custom_call" | custom-call | tf_op jit(solution)/shard_map/pallas_call | solution.py:550
  85.2 42.2 %shard_map.136 = (f32[64,8,128]{2,1,0:T(8,128)}, f32[3,3584]{1,0:T(4,128)}) custom-call(f32[64,8,128]{2,1,0:T(8,128)} %get-tuple-element.19.packed_ref, f32[8,24,128]{2,1,0:T(8,128)} %bitcast.9, f32[18,3584]{1,0:T(8,128)} %ja_ref.5, f32[3,3584]{1,0:T(4,128)} %get-tuple-element.20.y_ref.refs_2_, s32[1,3584]{1,0:T(1,128)} %broadcast_in_dim.18.ia_ref), custom_call_target="tpu_custom_call" | custom-call | tf_op jit(solution)/shard_map/pallas_call | solution.py:537
  127.5 2.1 %shard_map.137 = (f32[3,3584]{1,0:T(4,128)}, f32[8,128]{1,0:T(8,128)}) custom-call(s32[56]{0:T(128)} %multiply_add_fusion.1.places_ref.refs_0_, f32[64,8,128]{2,1,0:T(8,128)} %get-tuple-element.21.ret_ref, f32[3,3584]{1,0:T(4,128)} %get-tuple-element.22.near_ref, f32[18,3584]{1,0:T(8,128)} %refs_7_.3, f32[3,3584]{1,0:T(4,128)} %comp_ref.3, ...), custom_call_target="tpu_custom_call" | custom-call | tf_op jit(solution)/shard_map/pallas_call | solution.py:538
  129.6 17.2 %shard_map.138.refs_1_ = f32[8,128]{1,0:T(8,128)} custom-call(f32[8,128]{1,0:T(8,128)} %get-tuple-element.23.sums_ref), custom_call_target="tpu_custom_call" | custom-call | tf_op jit(solution)/shard_map/pallas_call | solution.py:542
  146.8 2.4 %shard_map.139 = (f32[3,3584]{1,0:T(4,128)}, f32[3,3584]{1,0:T(4,128)}, f32[64,8,128]{2,1,0:T(8,128)}) custom-call(s32[56]{0:T(128)} %multiply_add_fusion.1.places_ref.refs_0_, f32[8,128]{1,0:T(8,128)} %shard_map.138.refs_1_, f32[3,3584]{1,0:T(4,128)} %get-tuple-element.20.y_ref.refs_2_, f32[3,3584]{1,0:T(4,128)} %get-tuple-element.24.refs_3_, ...), custom_call_target="tpu_custom_call" | custom-call | tf_op jit(solution)/shard_map/pallas_call | solution.py:550
  149.2 30.0 %shard_map.140 = f32[8,24,128]{2,1,0:T(8,128)} custom-call(f32[64,8,128]{2,1,0:T(8,128)} %get-tuple-element.27.packed_ref, f32[8,24,128]{2,1,0:T(8,128)} %bitcast.10, f32[18,3584]{1,0:T(8,128)} %ja_ref.5, f32[3,3584]{1,0:T(4,128)} %get-tuple-element.13.y_ref, s32[1,3584]{1,0:T(1,128)} %broadcast_in_dim.18.ia_ref), custom_call_target="tpu_custom_call" | custom-call | tf_op jit(solution)/shard_map/pallas_call | solution.py:554
  179.2 1.0 copy.17
  180.3 0.8 copy-done
  181.1 0.7 multiply_add_fusion
  (10 shorter events, 0.2 us)
Async XLA Ops:
  0.6 0.7 copy-start.5
  1.5 1.9 %copy-start.2 = (s32[3584]{0:T(1024)S(1)}, s32[3584]{0:T(1024)}, u32[]{:S(2)}) copy-start(s32[3584]{0:T(1024)} %param.20) | copy-start | bytes 43012
  3.3 0.7 copy-start.3
  4.1 0.7 copy-start.4
  179.2 1.1 copy-start.1
  180.2 0.9 copy-start

commit v4 on v3

--- a/solution.py
+++ b/solution.py
@@ -241,12 +241,19 @@
     mine = lax.axis_index("contact_0") * 2 + lax.axis_index("contact_1")
     peers = [lax.rem(mine + k, n) for k in range(1, n)]
 
+    def offset(i, n):
+        far = (i + 1) // 2
+        return lax.rem(far * (1 - 2 * lax.rem(i + 1, 2)) + n, n)
+
     def to(k):
-        return lax.rem(body + k // groups, bodies), lax.rem(group + lax.rem(k, groups), groups)
+        b = offset(k // groups, bodies)
+        g = offset(lax.rem(k, groups), groups)
+        return lax.rem(body + b, bodies), lax.rem(group + g, groups)
 
     def source(k):
-        b = lax.rem(body - k // groups + bodies, bodies)
-        return b, lax.rem(group - lax.rem(k, groups) + groups, groups)
+        b = offset(k // groups, bodies)
+        g = offset(lax.rem(k, groups), groups)
+        return lax.rem(body - b + bodies, bodies), lax.rem(group - g + groups, groups)
 
     def name(b, g):
         return {"body": b, "group": g}
@@ -267,7 +274,7 @@
 
         lax.fori_loop(low, high, turn, 0)
 
-    loop(1, shards, lambda k: signal(name(*to(k))))
+    loop(1, shards, lambda k: signal(name(*to(shards - k))))
     for p in peers:
         signal(contact_id(p))
 
@@ -281,7 +288,7 @@
     loop(0, ia_ref.shape[1] // CHUNK, near)
     pl.semaphore_wait(pltpu.get_barrier_semaphore(), shards - 1 + n - 1)
 
-    loop(1, shards, lambda k: going(k).start())
+    loop(1, shards, lambda k: going(shards - k).start())
     recv_ref[0] = packed_ref[me]
 
     def far(i, first=0):
@@ -355,17 +362,16 @@
         for k in range(first, WIDE):
             backing(WIDE * i + k).start()
 
-    find(0)
-    find(1)
+    last = shards // WIDE - 1
+    find(last)
+
+    def find_give(i):
+        find(last - i)
+        give(last - i + 1)
+
+    loop(1, last + 1, find_give)
+    ret_ref[me] = back_ref[0]
     give(0, 1)
-
-    def find_give(i):
-        find(i)
-        give(i - 1)
-
-    loop(2, shards // WIDE, find_give)
-    ret_ref[me] = back_ref[0]
-    give(shards // WIDE - 1)
 
     def near_find(i):
         at = pl.ds(pl.multiple_of(i * CHUNK, CHUNK), CHUNK)

time: 182 us -> 182 us (level)
  no operation moved by 1% of the time
where the time goes in v4:
time: 182 us
  Pallas kernels  171 us (94%)
  local copies, waits for them, and re-layouts  8.16 us (4%)
    pallas_call x2, Pallas kernels, on_device(): returned, near = middle(packed, mass, jacobian_a, current, index_a)  95 us
    pallas_call x2, Pallas kernels, on_device(): sums = add_up(sums)  34.4 us
    pallas_call x1, Pallas kernels, on_device(): full = ending(packed, mass, jacobian_a, latest, index_a)  30.9 us
    pallas_call x2, Pallas kernels, on_device(): step(places, sums, current, gradient, latest, mu, active, jacobian_b, ind...  4.76 us
    pallas_call x2, Pallas kernels, on_device(): gradient_call(places, returned, near, jacobian_b, compliance, free_gap, c...  4.25 us

profile of v4, /device:TPU:1, one launch (start us, length us, event | category | flops | bytes accessed | tf_op | source)
XLA Modules:
  0.0 181.5 jit_solution(13296464995579736570)
XLA Ops:
  0.6 0.6 copy-done.5
  1.3 0.2 select_reduce_fusion
  1.5 0.5 multiply_add_fusion.1.places_ref.refs_0_
  2.0 1.3 broadcast_in_dim.18.ia_ref
  3.3 0.6 broadcast_in_dim.17.ib_ref.refs_8_
  4.1 0.6 broadcast_in_dim.20.refs_5_
  4.7 0.1 copy-done.4
  4.8 0.6 broadcast_in_dim.21.refs_6_
  5.4 1.0 reshape.17
  6.4 0.6 copy.16
  7.0 2.0 %shard_map.131.packed_ref = f32[64,8,128]{2,1,0:T(8,128)} custom-call(s32[56]{0:T(128)} %multiply_add_fusion.1.places_ref.refs_0_, f32[18,3584]{1,0:T(8,128)} %refs_7_.3, f32[3,3584]{1,0:T(4,128)} %yp_ref.1, s32[1,3584]{1,0:T(1,128)} %broadcast_in_dim.17.ib_ref.refs_8_), custom_call_target="tpu_custom_call" | custom-call | tf_op jit(solution)/shard_map/pallas_call | solution.py:541
  9.0 53.0 %shard_map.132 = (f32[64,8,128]{2,1,0:T(8,128)}, f32[3,3584]{1,0:T(4,128)}) custom-call(f32[64,8,128]{2,1,0:T(8,128)} %shard_map.131.packed_ref, f32[8,24,128]{2,1,0:T(8,128)} %bitcast.8, f32[18,3584]{1,0:T(8,128)} %ja_ref.5, f32[3,3584]{1,0:T(4,128)} %yp_ref.1, s32[1,3584]{1,0:T(1,128)} %broadcast_in_dim.18.ia_ref), custom_call_target="tpu_custom_call" | custom-call | tf_op jit(solution)/shard_map/pallas_call | solution.py:543
  62.0 0.6 broadcast_in_dim.19.yp_ref
  62.6 2.1 %shard_map.133 = (f32[3,3584]{1,0:T(4,128)}, f32[8,128]{1,0:T(8,128)}) custom-call(s32[56]{0:T(128)} %multiply_add_fusion.1.places_ref.refs_0_, f32[64,8,128]{2,1,0:T(8,128)} %get-tuple-element.15.ret_ref, f32[3,3584]{1,0:T(4,128)} %get-tuple-element.16.near_ref, f32[18,3584]{1,0:T(8,128)} %refs_7_.3, f32[3,3584]{1,0:T(4,128)} %comp_ref.3, ...), custom_call_target="tpu_custom_call" | custom-call | tf_op jit(solution)/shard_map/pallas_call | solution.py:544
  64.7 17.5 %shard_map.134.refs_1_ = f32[8,128]{1,0:T(8,128)} custom-call(f32[8,128]{1,0:T(8,128)} %get-tuple-element.17.sums_ref), custom_call_target="tpu_custom_call" | custom-call | tf_op jit(solution)/shard_map/pallas_call | solution.py:548
  82.2 2.4 %shard_map.135 = (f32[3,3584]{1,0:T(4,128)}, f32[3,3584]{1,0:T(4,128)}, f32[64,8,128]{2,1,0:T(8,128)}) custom-call(s32[56]{0:T(128)} %multiply_add_fusion.1.places_ref.refs_0_, f32[8,128]{1,0:T(8,128)} %shard_map.134.refs_1_, f32[3,3584]{1,0:T(4,128)} %yp_ref.1, f32[3,3584]{1,0:T(4,128)} %get-tuple-element.18.refs_3_.gp_ref, f32[3,3584]{1,0:T(4,128)} %yp_ref.1, ...), custom_call_target="tpu_custom_call" | custom-call | tf_op jit(solution)/shard_map/pallas_call | solution.py:556
  84.6 42.0 %shard_map.136 = (f32[64,8,128]{2,1,0:T(8,128)}, f32[3,3584]{1,0:T(4,128)}) custom-call(f32[64,8,128]{2,1,0:T(8,128)} %get-tuple-element.19.packed_ref, f32[8,24,128]{2,1,0:T(8,128)} %bitcast.9, f32[18,3584]{1,0:T(8,128)} %ja_ref.5, f32[3,3584]{1,0:T(4,128)} %get-tuple-element.20.y_ref.refs_2_, s32[1,3584]{1,0:T(1,128)} %broadcast_in_dim.18.ia_ref), custom_call_target="tpu_custom_call" | custom-call | tf_op jit(solution)/shard_map/pallas_call | solution.py:543
  126.7 2.1 %shard_map.137 = (f32[3,3584]{1,0:T(4,128)}, f32[8,128]{1,0:T(8,128)}) custom-call(s32[56]{0:T(128)} %multiply_add_fusion.1.places_ref.refs_0_, f32[64,8,128]{2,1,0:T(8,128)} %get-tuple-element.21.ret_ref, f32[3,3584]{1,0:T(4,128)} %get-tuple-element.22.near_ref, f32[18,3584]{1,0:T(8,128)} %refs_7_.3, f32[3,3584]{1,0:T(4,128)} %comp_ref.3, ...), custom_call_target="tpu_custom_call" | custom-call | tf_op jit(solution)/shard_map/pallas_call | solution.py:544
  128.8 16.8 %shard_map.138.refs_1_ = f32[8,128]{1,0:T(8,128)} custom-call(f32[8,128]{1,0:T(8,128)} %get-tuple-element.23.sums_ref), custom_call_target="tpu_custom_call" | custom-call | tf_op jit(solution)/shard_map/pallas_call | solution.py:548
  145.6 2.4 %shard_map.139 = (f32[3,3584]{1,0:T(4,128)}, f32[3,3584]{1,0:T(4,128)}, f32[64,8,128]{2,1,0:T(8,128)}) custom-call(s32[56]{0:T(128)} %multiply_add_fusion.1.places_ref.refs_0_, f32[8,128]{1,0:T(8,128)} %shard_map.138.refs_1_, f32[3,3584]{1,0:T(4,128)} %get-tuple-element.20.y_ref.refs_2_, f32[3,3584]{1,0:T(4,128)} %get-tuple-element.24.refs_3_, ...), custom_call_target="tpu_custom_call" | custom-call | tf_op jit(solution)/shard_map/pallas_call | solution.py:556
  148.0 30.9 %shard_map.140 = f32[8,24,128]{2,1,0:T(8,128)} custom-call(f32[64,8,128]{2,1,0:T(8,128)} %get-tuple-element.27.packed_ref, f32[8,24,128]{2,1,0:T(8,128)} %bitcast.10, f32[18,3584]{1,0:T(8,128)} %ja_ref.5, f32[3,3584]{1,0:T(4,128)} %get-tuple-element.13.y_ref, s32[1,3584]{1,0:T(1,128)} %broadcast_in_dim.18.ia_ref), custom_call_target="tpu_custom_call" | custom-call | tf_op jit(solution)/shard_map/pallas_call | solution.py:560
  178.9 1.0 copy.17
  180.0 0.8 copy-done
  180.8 0.7 multiply_add_fusion
  (10 shorter events, 0.2 us)
Async XLA Ops:
  0.6 0.7 copy-start.5
  1.5 1.9 %copy-start.2 = (s32[3584]{0:T(1024)S(1)}, s32[3584]{0:T(1024)}, u32[]{:S(2)}) copy-start(s32[3584]{0:T(1024)} %param.20) | copy-start | bytes 43012
  3.3 0.7 copy-start.3
  4.1 0.7 copy-start.4
  178.9 1.1 copy-start.1
  179.9 0.9 copy-start
